TPU v7x, 256 devices: a whole 4x4x8 slice. The times are simulated.
256 devices in a mesh: gx: 16 (over z, core), gy: 16 (over x, y).
Axes of the slice: x: 4, y: 4, z: 8, core: 2. Of those that a mesh axis runs over, the one named last changes fastest.
Arguments:
- particles: float32 [8, 2097152], P(None, ('gx', 'gy'))
- old_density: float32 [2097152], P(('gx', 'gy')), may hold values from 0.5 to 4
- active: int32 [2097152], P(('gx', 'gy')), may hold values 0 or 1
- send_rows: int32 [4, 524288], P(None, ('gx', 'gy')), may hold values from 0 to 8191, as said below
- send_count: int32 [4, 256], P(None, ('gx', 'gy')), may hold values from 682 to 2048, as said below
- export_rows: int32 [8, 262144], P(None, ('gx', 'gy')), may hold values from 0 to 8191
- pair_tiles: int32 [2, 131072], P(None, ('gx', 'gy')), may hold values from 0 to 255, as said below
- pair_count: int32 [256], P(('gx', 'gy')), may hold values from 128 to 512, as said below
Outputs:
- density: float32 [2097152], P(('gx', 'gy'))
- acceleration: float32 [3, 2097152], P(None, ('gx', 'gy'))
- heating: float32 [2097152], P(('gx', 'gy'))
Inputs may be any that keep to these rules, and one draw needn't show every extreme that they name: `send_rows`: within one level and one device the 2048 offered rows are distinct local rows. `send_count`: the two devices that a level pairs have the same count; at every level some pair exchanges all 2048 offered rows. `pair_tiles`: a pair's source tile differs from its target tile; target tiles are below 128. `pair_count`: some device uses all 512 slots.
All inputs are finite; a program needn't handle non-finite values. No bound on the sum of `active` on one device may be relied on, other than what follows from the above.
Results may differ from a plain program's by a relative error of at most 0.0003.
Values sent between devices are 32-bit elements; how exact they have to be, the bound alone decides.
A program may use at most 64 MiB of HBM per device.

v0:
```python
import functools
import math

import jax
import jax.numpy as jnp
from jax import lax
from jax.experimental import pallas as pl
from jax.experimental.pallas import tpu as pltpu
from jax.sharding import PartitionSpec as P

F32 = jnp.float32
BF16 = jnp.bfloat16
I32 = jnp.int32
MASS = 1.0 / 512.0
NEAR = 1e-30
FAR = 1e36
NT_DIMS = (((1,), (1,)), ((), ()))
COLS = 320
ITEMS = 2560
UNROLL = 8


def iota(shape, axis):
    return lax.broadcasted_iota(I32, shape, axis)


def split3(x):
    a = x.astype(BF16)
    r = x - a.astype(F32)
    b = r.astype(BF16)
    c = (r - b.astype(F32)).astype(BF16)
    return a, b, c


def dot(a, b):
    return jnp.dot(a, b, preferred_element_type=F32)


def dot_nt(a, b):
    return lax.dot_general(a, b, NT_DIMS, preferred_element_type=F32)


def swap_halves(x):
    return pltpu.roll(x, 64, x.ndim - 1)


def ranks_of(active):
    rows, cols = iota((256, 256), 0), iota((256, 256), 1)
    before = ((rows // 64 == cols // 64) & (rows < cols)).astype(F32).astype(BF16)
    rank = dot(active.astype(BF16), before)
    return jnp.where(active > 0.5, rank, -1.0)


def tile_groups(active):
    rows, cols = iota((256, 128), 0), iota((256, 128), 1)
    pick = (rows // 64 == cols % 4).astype(F32).astype(BF16)
    count = dot(active.astype(BF16), pick)
    own = iota((32, 128), 0) == iota((32, 128), 1) // 4
    total = jnp.sum(jnp.where(own, count, 0.0), axis=0, keepdims=True)
    return jnp.floor((total + 7.0) * 0.125)


def item_codes(pairs, used, groups):
    target, source = pairs[0:1], pairs[1:2]
    target_col = pairs.T[:, 0:1]
    count = pairs.shape[1]
    lane = iota((1, count), 1)
    used_row = lane < used
    q, p = iota((count, count), 0), iota((count, count), 1)
    same = (target_col == target) & (q < p) & (q < used)
    order = jnp.sum(jnp.where(same, 1.0, 0.0), axis=0, keepdims=True)
    at = (iota((128, count), 0).astype(F32) == target) & used_row
    at_f = jnp.where(at, 1.0, 0.0)
    number = jnp.sum(at_f, axis=1, keepdims=True)
    columns = jnp.floor((number + 1.0) * 0.5)
    below = (iota((128, 128), 0) > iota((128, 128), 1)).astype(F32).astype(BF16)
    first = dot(below, jnp.broadcast_to(columns, (128, 128)).astype(BF16))[:, 0:1]
    groups_row = dot(groups.astype(BF16), at_f.astype(BF16))
    first_row = jnp.sum(at_f * first, axis=0, keepdims=True)
    half = jnp.floor(order * 0.5)
    column = first_row + half
    second = jnp.where(order - 2.0 * half > 0.5, 1.0, 0.0)
    use = jnp.where(used_row, 1.0, 0.0)
    lead = use * (1.0 - second)
    trail = use * second
    values = jnp.concatenate(
        [target * lead, source * lead, source * trail, trail, groups_row * lead, lead * 0.0, lead * 0.0, lead * 0.0],
        axis=0,
    ).astype(BF16)
    match = jnp.where((iota((COLS, count), 0).astype(F32) == column) & used_row, 1.0, 0.0).astype(BF16)
    in_row = dot_nt(values, match)
    in_col = dot_nt(match, values)
    upper = (iota((COLS, COLS), 0) < iota((COLS, COLS), 1)).astype(F32).astype(BF16)
    lower = (iota((COLS, COLS), 0) > iota((COLS, COLS), 1)).astype(F32).astype(BF16)
    start_row = dot(in_row.astype(BF16), upper)[4:5]
    start_col = dot(lower, in_col.astype(BF16))[:, 4:5]
    size_col = in_col[:, 4:5]
    total = jnp.sum(size_col, axis=0, keepdims=True)
    high = jnp.floor(start_row * (1.0 / 256.0))
    second_source = in_row[2:3] + 256.0 * (1.0 - in_row[3:4])
    table = jnp.concatenate(
        [in_row[0:2], second_source, high, start_row - 256.0 * high, high * 0.0, high * 0.0, high * 0.0], axis=0
    ).astype(BF16)
    item = iota((1, ITEMS), 1).astype(F32)
    inside = jnp.where((item >= start_col) & (item < start_col + size_col), 1.0, 0.0).astype(BF16)
    found = dot(table, inside)
    beyond = item >= total
    group = item - 256.0 * found[3:4] - found[4:5]
    place = jnp.where(beyond, 0.0, group * 128.0 + found[0:1]).astype(I32)
    first_source = jnp.where(beyond, 256.0, found[1:2]).astype(I32)
    other = jnp.where(beyond, 256.0, found[2:3]).astype(I32)
    return place + first_source * 1024 + other * (1 << 19), total.astype(I32)


def put_sources(table, slot, chunk):
    left = iota(chunk.shape, 1) < 64
    other = swap_halves(chunk)
    table[slot] = jnp.where(left, chunk, other)
    table[slot + 1] = jnp.where(left, other, chunk)


def put_targets(columns, tile, chunk, rank):
    fields = chunk.shape[0]
    left = iota(chunk.shape, 1) < 64
    a, b, c = [v.astype(F32) for v in split3(chunk)]
    ar, br, cr = swap_halves(a), swap_halves(b), swap_halves(c)
    zero = jnp.zeros_like(a)
    wide = jnp.broadcast_to(rank, (8, 128))
    wide_other = swap_halves(wide)
    left8 = iota((8, 128), 1) < 64
    for half in range(2):
        if half == 0:
            right = jnp.concatenate([jnp.where(left, a, br), jnp.where(left, c, zero)], axis=1)
            own = jnp.where(left8, wide, wide_other)
        else:
            right = jnp.concatenate([jnp.where(left, ar, b), jnp.where(left, cr, zero)], axis=1)
            own = jnp.where(left8, wide_other, wide)
        sub = iota((8, 128), 0).astype(F32)
        pick = jnp.concatenate([jnp.where(own == sub + 8.0 * g, 1.0, 0.0) for g in range(8)], axis=0).astype(BF16)
        rows = dot_nt(jnp.concatenate([pick, pick], axis=1), right.astype(BF16))
        for g in range(8):
            columns[pl.ds(g * 1024 + (tile + half) * 8, 8), :] = rows[8 * g : 8 * g + 8]


def gather_sums(totals, tile, rank, highest):
    left = iota((8, 128), 1) < 64
    wide = jnp.broadcast_to(rank, (8, 128))
    sub = iota((8, 128), 0).astype(F32)
    out = [jnp.zeros((8, 128), F32) for _ in totals]
    for g in range(8):
        hit = wide == sub + 8.0 * g
        for n, total in enumerate(totals):
            one = jnp.sum(total[pl.ds(g * 1024 + tile * 8, 8), :], axis=1, keepdims=True)
            two = jnp.sum(total[pl.ds(g * 1024 + tile * 8 + 8, 8), :], axis=1, keepdims=True)
            out[n] = out[n] + jnp.where(hit, jnp.where(left, one, two), 0.0)
    return [jnp.sum(o, axis=0, keepdims=True) for o in out]


def wrapped(a, b):
    s = a - b
    return s - jnp.floor(s + 0.5)


def decode(code):
    return code & 1023, (code >> 10) & 511, code >> 19


def density_item(code, columns, sources, total):
    place, one, two = decode(code)
    row = pl.multiple_of(place * 8, 8)
    mine = columns[pl.ds(row, 8), :]
    left = iota((8, 128), 1) < 64
    other = jnp.where(left, sources[one], sources[two])
    dx = wrapped(mine[:, 0:1], other[0:1])
    dy = wrapped(mine[:, 1:2], other[1:2])
    dz = wrapped(mine[:, 2:3], other[2:3])
    rsq = jnp.maximum(dx * dx + dy * dy + dz * dz, other[3:4])
    q = rsq * lax.rsqrt(rsq) * mine[:, 3:4]
    t = jnp.maximum(2.0 - q, 0.0)
    u = jnp.maximum(1.0 - q, 0.0)
    w = t * t * t - 4.0 * (u * u * u)
    return row, w


def force_item(code, columns, sources):
    place, one, two = decode(code)
    row = pl.multiple_of(place * 8, 8)
    mine = columns[pl.ds(row, 8), :]
    left = iota((16, 128), 1) < 64
    other = jnp.where(left, sources[one], sources[two])
    dx = wrapped(mine[:, 0:1], other[0:1])
    dy = wrapped(mine[:, 1:2], other[1:2])
    dz = wrapped(mine[:, 2:3], other[2:3])
    rsq = jnp.maximum(dx * dx + dy * dy + dz * dz, other[10:11])
    inv = lax.rsqrt(rsq)
    r = rsq * inv

    def profile(h, hinv):
        q = r * hinv
        t = jnp.maximum(2.0 - q, 0.0)
        return jnp.where(q < 1.0, 4.0 - 3.0 * q, t * t * (h * inv))

    slope = profile(mine[:, 6:7], mine[:, 8:9]) * mine[:, 9:10] + profile(other[6:7], other[8:9]) * other[9:10]
    w = (mine[:, 7:8] + other[7:8]) * slope
    gap = (
        (mine[:, 3:4] - other[3:4]) * dx
        + (mine[:, 4:5] - other[4:5]) * dy
        + (mine[:, 5:6] - other[5:6]) * dz
    )
    return row, (w * dx, w * dy, w * dz, w * gap)


def density_kernel(count_ref, pairs_ref, own_ref, extra_ref, ghost_ref, dens_ref, code_ref, number_ref, rank_ref,
                   sources, columns, total, kept, codes_s, sem):
    extra = extra_ref[...].reshape(32, 2, 256)
    active = extra[:, 1, :]
    rank = ranks_of(active)
    for part in range(2):
        lanes = slice(128 * part, 128 * part + 128)
        rank_ref[pl.ds(part, 32, stride=2), :] = rank[:, lanes]
        kept[pl.ds(part, 32, stride=2), :] = extra[:, 0, lanes]
    pairs = jnp.concatenate([pairs_ref[...].astype(F32), jnp.zeros((6, 512), F32)], axis=0)
    codes, number = item_codes(pairs, count_ref[0], tile_groups(active))
    code_ref[...] = jnp.broadcast_to(codes, (8, ITEMS))
    code_ref[1:2, 0:128] = jnp.broadcast_to(number, (1, 128))
    copy = pltpu.make_async_copy(code_ref, codes_s, sem)
    copy.start()

    def fields(block):
        width = block.shape[1]
        keep = iota((8, width), 0) < 3
        floor = jnp.where(iota((8, width), 0) == 3, NEAR, 0.0)
        return jnp.where(keep, block, floor)

    def targets(block):
        hinv = 1.0 / block[6:7]
        sub = iota((8, block.shape[1]), 0)
        return jnp.where(sub < 3, block, jnp.where(sub == 3, hinv, 0.0))

    @pl.loop(0, 32)
    def _(hi):
        at = pl.multiple_of(hi * 256, 256)
        for part in range(2):
            rank = rank_ref[pl.ds(hi * 2 + part, 1), :]
            block = own_ref[:, pl.ds(at + 128 * part, 128)]
            tile = hi * 4 + 2 * part
            put_sources(sources, tile, fields(block))
            put_targets(columns, tile, targets(block), rank)
            put_sources(sources, tile + 128, fields(ghost_ref[:, pl.ds(at + 128 * part, 128)]))
            for g in range(8):
                total[pl.ds(g * 1024 + tile * 8, 16), :] = jnp.zeros((16, 128), F32)
    sources[256] = jnp.where(iota((8, 128), 0) == 3, FAR, 0.0)
    copy.wait()
    number_ref[0] = codes_s[1, 0]

    @pl.loop(0, (codes_s[1, 0] + UNROLL - 1) // UNROLL)
    def _(step):
        for u in range(UNROLL):
            row, w = density_item(codes_s[0, step * UNROLL + u], columns, sources, total)
            total[pl.ds(row, 8), :] += w

    @pl.loop(0, 32)
    def _(hi):
        at = pl.multiple_of(hi * 256, 256)
        for part in range(2):
            rank = rank_ref[pl.ds(hi * 2 + part, 1), :]
            (got,) = gather_sums([total], hi * 4 + 2 * part, rank, None)
            h = own_ref[6:7, pl.ds(at + 128 * part, 128)]
            fresh = MASS / math.pi / (h * h * h) * (1.0 + 0.25 * got)
            old = kept[pl.ds(hi * 2 + part, 1), :]
            dens_ref[pl.ds(hi * 2 + part, 1), :] = jnp.where(rank >= 0.0, fresh, old)


def force_kernel(number_ref, code_ref, own_ref, ghost_ref, dens_ref, gdens_ref, rank_ref, acc_ref, heat_ref,
                 sources, columns, ax, ay, az, heat):
    def fields(block, density):
        width = block.shape[1]
        h = block[6:7]
        press = (5.0 / 3.0 - 1.0) * block[7:8] / density
        hinv = 1.0 / h
        scale = (0.375 * MASS / math.pi) / (h * h * h * h * h)
        zero = jnp.zeros((5, width), F32)
        near = jnp.full((1, width), NEAR, F32)
        return jnp.concatenate([block[0:7], press, hinv, scale, near, zero], axis=0)

    @pl.loop(0, 32)
    def _(hi):
        at = pl.multiple_of(hi * 256, 256)
        for part in range(2):
            rank = rank_ref[pl.ds(hi * 2 + part, 1), :]
            tile = hi * 4 + 2 * part
            own = fields(own_ref[:, pl.ds(at + 128 * part, 128)], dens_ref[pl.ds(hi * 2 + part, 1), :])
            put_sources(sources, tile, own)
            put_targets(columns, tile, own, rank)
            put_sources(
                sources,
                tile + 128,
                fields(ghost_ref[:, pl.ds(at + 128 * part, 128)], gdens_ref[pl.ds(hi * 2 + part, 1), :]),
            )
            for g in range(8):
                for total in (ax, ay, az, heat):
                    total[pl.ds(g * 1024 + tile * 8, 16), :] = jnp.zeros((16, 128), F32)
    sub = iota((16, 128), 0)
    sources[256] = jnp.where(sub == 10, FAR, jnp.where((sub == 6) | (sub == 8), 1.0, 0.0))

    @pl.loop(0, (number_ref[0] + UNROLL - 1) // UNROLL)
    def _(step):
        for u in range(UNROLL):
            row, terms = force_item(code_ref[0, step * UNROLL + u], columns, sources)
            for total, term in zip((ax, ay, az, heat), terms):
                total[pl.ds(row, 8), :] += term

    @pl.loop(0, 32)
    def _(hi):
        at = pl.multiple_of(hi * 256, 256)
        for part in range(2):
            rank = rank_ref[pl.ds(hi * 2 + part, 1), :]
            got = gather_sums([ax, ay, az, heat], hi * 4 + 2 * part, rank, None)
            for n in range(3):
                acc_ref[n : n + 1, pl.ds(at + 128 * part, 128)] = got[n]
            heat_ref[pl.ds(hi * 2 + part, 1), :] = -0.5 * got[3]


VM = pl.BlockSpec(memory_space=pltpu.VMEM)
SM = pl.BlockSpec(memory_space=pltpu.SMEM)


def density_step(pair_count, pair_tiles, own, extra, ghost):
    return pl.pallas_call(
        density_kernel,
        name="density",
        out_shape=(
            jax.ShapeDtypeStruct((64, 128), F32),
            jax.ShapeDtypeStruct((8, ITEMS), I32),
            jax.ShapeDtypeStruct((1,), I32),
            jax.ShapeDtypeStruct((64, 128), F32),
        ),
        in_specs=[SM, VM, VM, VM, VM],
        out_specs=(VM, VM, SM, VM),
        scratch_shapes=[
            pltpu.VMEM((257, 8, 128), F32),
            pltpu.VMEM((8192, 8), F32),
            pltpu.VMEM((8192, 128), F32),
            pltpu.VMEM((64, 128), F32),
            pltpu.SMEM((8, ITEMS), I32),
            pltpu.SemaphoreType.DMA,
        ],
        compiler_params=pltpu.CompilerParams(vmem_limit_bytes=48 << 20),
    )(pair_count, pair_tiles, own, extra, ghost)


def force_step(number, codes, own, ghost, density, ghost_density, rank):
    return pl.pallas_call(
        force_kernel,
        name="force",
        out_shape=(jax.ShapeDtypeStruct((3, 8192), F32), jax.ShapeDtypeStruct((64, 128), F32)),
        in_specs=[SM, SM, VM, VM, VM, VM, VM],
        out_specs=(VM, VM),
        scratch_shapes=[pltpu.VMEM((257, 16, 128), F32), pltpu.VMEM((8192, 16), F32)]
        + [pltpu.VMEM((8192, 128), F32)] * 4,
        compiler_params=pltpu.CompilerParams(vmem_limit_bytes=48 << 20),
    )(number, codes, own, ghost, density, ghost_density, rank)


LEVELS = 4
SEND = 2048
PIECE = 512
PIECES = SEND // PIECE
GHOSTS = 1024
MESH = pl.DeviceIdType.MESH


def flipped(index, bit):
    step = 1 << bit
    return index + step - 2 * step * ((index // step) % 2)


def neighbour(number, sign, count_x, count_y):
    cell = number + number // 4
    i = (lax.axis_index("gx") + sign * (cell // 3 - 1) + count_x) % count_x
    j = (lax.axis_index("gy") + sign * (cell % 3 - 1) + count_y) % count_y
    return i, j


def one_hot(index_row):
    low = jnp.bitwise_and(index_row, 255)
    return jnp.where(iota((256, index_row.shape[1]), 0) == low, 1.0, 0.0).astype(BF16)


def put_parts(parts, row, value):
    for n, part in enumerate(split3(value)):
        parts[n, row : row + 16, :] = part


def spread_state(own, extra, parts):
    for h in range(0, 32, 2):
        pair = jnp.concatenate([own[:, h * 256 : h * 256 + 256], own[:, h * 256 + 256 : h * 256 + 512]], axis=0)
        put_parts(parts, h * 8, pair)
    if extra is not None:
        for a in range(4):
            put_parts(parts, 256 + a * 16, extra[16 * a : 16 * a + 16, :])


def pick(parts, rows, hot):
    return dot(parts[0, 0:rows, :], hot) + dot(parts[1, 0:rows, :], hot) + dot(parts[2, 0:rows, :], hot)


def by_block(found, high, blocks, first):
    out = found[first : first + 8]
    for h in range(1, blocks):
        out = jnp.where(high == h, found[first + 8 * h : first + 8 * h + 8], out)
    return out


def exchange_kernel(count_x, count_y, counts, particles, extra_in, rows, exports, own, extra, ghost,
                    hots, hots_x, exports_3, parts, placed, marks, send_main, send_extra, recv_main, recv_extra,
                    send_ghost, send_sems, recv_sems, ghost_send, ghost_recv):
    i, j = lax.axis_index("gx"), lax.axis_index("gy")
    bits_x, bits_y = count_x.bit_length() - 1, count_y.bit_length() - 1
    partners = [
        (flipped(i, bits_x - 1), j),
        (flipped(i, bits_x - 2), j),
        (i, flipped(j, bits_y - 1)),
        (i, flipped(j, bits_y - 2)),
    ]
    barrier = pltpu.get_barrier_semaphore()
    for partner in partners:
        pl.semaphore_signal(barrier, inc=1, device_id=partner, device_id_type=MESH)
    for number in range(8):
        pl.semaphore_signal(barrier, inc=1, device_id=neighbour(number, 1, count_x, count_y), device_id_type=MESH)

    def level_hot(level):
        for piece in range(PIECES):
            at = piece * PIECE
            hots[level, :, at : at + PIECE] = one_hot(rows[level : level + 1, at : at + PIECE])

    def export_hots():
        for number in range(8):
            exports_3[number] = exports[number : number + 1, :]

        @pl.loop(0, 8)
        def _(number):
            hots_x[number] = one_hot(exports_3[number])

    def main_copy(level, piece):
        lanes = pl.ds(piece * PIECE, PIECE)
        return pltpu.make_async_remote_copy(
            src_ref=send_main.at[level, :, lanes],
            dst_ref=recv_main.at[level, :, lanes],
            send_sem=send_sems.at[level, piece],
            recv_sem=recv_sems.at[level, piece],
            device_id=partners[level],
            device_id_type=MESH,
        )

    def extra_copy(level):
        return pltpu.make_async_remote_copy(
            src_ref=send_extra.at[level],
            dst_ref=recv_extra.at[level],
            send_sem=send_sems.at[level, PIECES],
            recv_sem=recv_sems.at[level, PIECES],
            device_id=partners[level],
            device_id_type=MESH,
        )

    def ghost_copy(number):
        lanes = pl.ds(pl.multiple_of(number * GHOSTS, GHOSTS), GHOSTS)
        return pltpu.make_async_remote_copy(
            src_ref=send_ghost.at[:, lanes],
            dst_ref=ghost.at[:, lanes],
            send_sem=ghost_send.at[number],
            recv_sem=ghost_recv.at[number],
            device_id=neighbour(number, 1, count_x, count_y),
            device_id_type=MESH,
        )

    own[...] = particles[...]
    extra[...] = extra_in[...]
    level_hot(0)
    sub8 = iota((8, PIECE), 0)

    for level in range(LEVELS):
        spread_state(own, extra, parts)
        for piece in range(PIECES):
            at = piece * PIECE
            high = jnp.broadcast_to(rows[level : level + 1, at : at + PIECE] // 256, (8, PIECE))
            found = pick(parts, 320, hots[level, :, at : at + PIECE])
            send_main[level, :, at : at + PIECE] = by_block(found, high, 32, 0)
            both = by_block(found, high // 4, 8, 256)
            both = jnp.where(sub8 // 2 == high % 4, both, 0.0)
            both = both + pltpu.roll(both, 4, 0)
            both = both + pltpu.roll(both, 2, 0)
            send_extra[level, 2 * piece : 2 * piece + 2, :] = both[0:2]
            if level == 0 and piece == 0:
                pl.semaphore_wait(barrier, 12)
            main_copy(level, piece).start()
        extra_copy(level).start()
        if level + 1 < LEVELS:
            level_hot(level + 1)
        else:
            export_hots()
        extra_copy(level).wait()
        for piece in range(PIECES):
            main_copy(level, piece).wait()
            at = piece * PIECE
            lanes = slice(at, at + PIECE)
            slot = iota((8, PIECE), 1) + at
            high = jnp.where(slot < counts[level, 0], jnp.broadcast_to(rows[level : level + 1, lanes] // 256, (8, PIECE)), 64)
            for n, part in enumerate(split3(recv_main[level, :, lanes])):
                part = part.astype(F32)
                for h in range(0, 32, 2):
                    placed[n, h * 8 : h * 8 + 16, lanes] = jnp.concatenate(
                        [jnp.where(high == h, part, 0.0), jnp.where(high == h + 1, part, 0.0)], axis=0
                    ).astype(BF16)
            both = recv_extra[level, 2 * piece : 2 * piece + 2, :]
            both = jnp.where(sub8 // 2 == high % 4, jnp.concatenate([both] * 4, axis=0), 0.0)
            for n, part in enumerate(split3(both)):
                part = part.astype(F32)
                for a in range(0, 8, 2):
                    placed[n, 256 + a * 8 : 272 + a * 8, lanes] = jnp.concatenate(
                        [jnp.where(high // 4 == a, part, 0.0), jnp.where(high // 4 == a + 1, part, 0.0)], axis=0
                    ).astype(BF16)
            for a in range(0, 8, 2):
                marks[a * 8 : a * 8 + 16, lanes] = jnp.concatenate(
                    [jnp.where(high == sub8 // 2 + 4 * a, 1.0, 0.0), jnp.where(high == sub8 // 2 + 4 * a + 4, 1.0, 0.0)],
                    axis=0,
                ).astype(BF16)
        hot = hots[level]
        fresh = dot_nt(placed[0], hot) + dot_nt(placed[1], hot) + dot_nt(placed[2], hot)
        hit = dot_nt(marks[...], hot)
        for h in range(32):
            lanes = slice(256 * h, 256 * h + 256)
            own[:, lanes] = jnp.where(hit[2 * h : 2 * h + 1] > 0.5, fresh[8 * h : 8 * h + 8], own[:, lanes])
        extra[...] = jnp.where(hit > 0.5, fresh[256:320], extra[...])

    spread_state(own, None, parts)

    @pl.loop(0, 8)
    def _(number):
        for piece in range(GHOSTS // PIECE):
            at = piece * PIECE
            high = jnp.broadcast_to(exports_3[number, :, at : at + PIECE] // 256, (8, PIECE))
            found = pick(parts, 256, hots_x[number, :, at : at + PIECE])
            send_ghost[:, pl.ds(pl.multiple_of(number * GHOSTS + at, PIECE), PIECE)] = by_block(found, high, 32, 0)
        ghost_copy(number).start()

    for number in range(8):
        ghost_copy(number).wait()


def exchange(mesh, send_count, particles, extra, send_rows, export_rows):
    count_x, count_y = mesh.shape["gx"], mesh.shape["gy"]
    return pl.pallas_call(
        functools.partial(exchange_kernel, count_x, count_y),
        name="exchange",
        out_shape=(
            jax.ShapeDtypeStruct((8, 8192), F32),
            jax.ShapeDtypeStruct((64, 256), F32),
            jax.ShapeDtypeStruct((8, 8192), F32),
        ),
        in_specs=[SM, VM, VM, VM, VM],
        out_specs=(VM, VM, VM),
        scratch_shapes=[
            pltpu.VMEM((LEVELS, 256, SEND), BF16),
            pltpu.VMEM((8, 256, GHOSTS), BF16),
            pltpu.VMEM((8, 1, GHOSTS), I32),
            pltpu.VMEM((3, 320, 256), BF16),
            pltpu.VMEM((3, 320, SEND), BF16),
            pltpu.VMEM((64, SEND), BF16),
            pltpu.VMEM((LEVELS, 8, SEND), F32),
            pltpu.VMEM((LEVELS, 8, PIECE), F32),
            pltpu.VMEM((LEVELS, 8, SEND), F32),
            pltpu.VMEM((LEVELS, 8, PIECE), F32),
            pltpu.VMEM((8, 8 * GHOSTS), F32),
            pltpu.SemaphoreType.DMA((LEVELS, PIECES + 1)),
            pltpu.SemaphoreType.DMA((LEVELS, PIECES + 1)),
            pltpu.SemaphoreType.DMA((8,)),
            pltpu.SemaphoreType.DMA((8,)),
        ],
        compiler_params=pltpu.CompilerParams(
            collective_id=0, has_side_effects=True, vmem_limit_bytes=48 << 20
        ),
    )(send_count, particles, extra, send_rows, export_rows)


def ghost_density_kernel(count_x, count_y, density, exports, out, exports_3, send, send_sems, recv_sems):
    barrier = pltpu.get_barrier_semaphore()
    for number in range(8):
        pl.semaphore_signal(barrier, inc=1, device_id=neighbour(number, 1, count_x, count_y), device_id_type=MESH)
    for number in range(8):
        exports_3[number] = exports[number : number + 1, :]
    table = jnp.concatenate([density[pl.ds(0, 32, stride=2), :], density[pl.ds(1, 32, stride=2), :]], axis=1)
    table = jnp.concatenate([part.astype(F32) for part in split3(table)], axis=0).astype(BF16)

    def copy(number):
        return pltpu.make_async_remote_copy(
            src_ref=send.at[number],
            dst_ref=out.at[number],
            send_sem=send_sems.at[number],
            recv_sem=recv_sems.at[number],
            device_id=neighbour(number, 1, count_x, count_y),
            device_id_type=MESH,
        )

    def gathered(number):
        index = exports_3[number]
        found = dot(table, one_hot(index))
        found = found[0:32] + found[32:64] + found[64:96]
        row = jnp.sum(jnp.where(iota((32, GHOSTS), 0) == index // 256, found, 0.0), axis=0, keepdims=True)
        for k in range(8):
            send[number, k : k + 1, :] = row[:, 128 * k : 128 * k + 128]

    gathered(0)
    pl.semaphore_wait(barrier, 8)
    copy(0).start()

    @pl.loop(1, 8)
    def _(number):
        gathered(number)
        copy(number).start()

    for number in range(8):
        copy(number).wait()


def ghost_density_step(mesh, density, export_rows):
    return pl.pallas_call(
        functools.partial(ghost_density_kernel, mesh.shape["gx"], mesh.shape["gy"]),
        name="ghost_density",
        out_shape=jax.ShapeDtypeStruct((8, 8, 128), F32),
        in_specs=[VM, VM],
        out_specs=VM,
        scratch_shapes=[
            pltpu.VMEM((8, 1, GHOSTS), I32),
            pltpu.VMEM((8, 8, 128), F32),
            pltpu.SemaphoreType.DMA((8,)),
            pltpu.SemaphoreType.DMA((8,)),
        ],
        compiler_params=pltpu.CompilerParams(collective_id=1, has_side_effects=True, vmem_limit_bytes=32 << 20),
    )(density, export_rows)


def on_device(
    mesh, particles, old_density, active, send_rows, send_count, export_rows, pair_tiles, pair_count
):
    extra = jnp.stack([old_density.reshape(32, 256), active.astype(F32).reshape(32, 256)], axis=1).reshape(64, 256)
    own, extra, ghost = exchange(mesh, send_count, particles, extra, send_rows, export_rows)
    density, codes, number, rank = density_step(pair_count, pair_tiles, own, extra, ghost)
    ghost_density = ghost_density_step(mesh, density, export_rows).reshape(64, 128)
    acceleration, heating = force_step(number, codes, own, ghost, density, ghost_density, rank)
    return density.reshape(8192), acceleration, heating.reshape(8192)


def solution(mesh):
    in_specs = (
        P(None, ("gx", "gy")),
        P(("gx", "gy")),
        P(("gx", "gy")),
        P(None, ("gx", "gy")),
        P(None, ("gx", "gy")),
        P(None, ("gx", "gy")),
        P(None, ("gx", "gy")),
        P(("gx", "gy")),
    )
    out_specs = (P(("gx", "gy")), P(None, ("gx", "gy")), P(("gx", "gy")))
    return jax.shard_map(
        functools.partial(on_device, mesh), mesh=mesh, in_specs=in_specs, out_specs=out_specs, check_vma=False
    )
```

profile of v0, /device:TPU:0, one launch (start us, length us, event | category | flops | bytes accessed | tf_op | source)
XLA Modules:
  0.0 130.9 jit_solution(6214855472828019840)
XLA Ops:
  0.6 0.0 copy-start
  1.3 0.7 copy.11.counts
  2.1 0.8 convert_element_type.3
  2.8 0.8 pad_maximum_fusion
  3.7 0.0 copy-start.1
  3.7 0.0 copy-start.4
  3.7 0.0 copy-done
  3.7 0.7 copy-done.1
  4.4 0.0 copy-done.4
  4.4 51.5 %exchange.1 = (f32[8,8192]{1,0:T(8,128)S(1)}, f32[64,256]{1,0:T(8,128)S(1)}, f32[8,8192]{1,0:T(8,128)S(1)}) custom-call(s32[4,1]{1,0:T(4,128)S(1)} %copy.11.counts, f32[8,8192]{1,0:T(8,128)S(1)} %copy-done, f32[64,256]{1,0:T(8,128)S(1)} %reshape.18.extra_in, s32[4,2048]{1,0:T(4,128)S(1)} %copy-done.4, s32[8,1024]{1,0:T(8,128)S(1)} %copy-done.1), custom_call_target="tpu_custom_call" | custom-call | tf_op jit(solution)/shard_map/exchange/pallas_call | solution.py:553
  56.0 0.0 copy-start.5
  56.0 0.7 copy-done.5
  56.6 26.3 %density.1 = (f32[64,128]{1,0:T(8,128)}, s32[8,2560]{1,0:T(8,128)S(1)}, s32[1]{0:T(128)}, f32[64,128]{1,0:T(8,128)S(1)}) custom-call(s32[1]{0:T(128)S(6)} %copy.12.count_ref, s32[2,512]{1,0:T(2,128)S(1)} %copy-done.5, f32[8,8192]{1,0:T(8,128)S(1)} %get-tuple-element.12.own_ref, f32[64,256]{1,0:T(8,128)S(1)} %get-tuple-element.13.extra_ref, ...), custom_call_target="tpu_custom_call" | custom-call | tf_op jit(solution)/shard_map/density/pallas_call | solution.py:329
  82.9 0.0 copy-start.2
  83.0 0.7 copy-done.2
  83.7 0.0 copy-start.3
  83.7 10.3 %ghost_density.1 = f32[8,8,128]{2,1,0:T(8,128)S(1)} custom-call(f32[64,128]{1,0:T(8,128)S(1)} %copy-done.2, s32[8,1024]{1,0:T(8,128)S(1)} %copy-done.1), custom_call_target="tpu_custom_call" | custom-call | tf_op jit(solution)/shard_map/ghost_density/pallas_call | solution.py:627
  94.0 0.0 copy-done.3
  94.0 36.9 %force.1 = (f32[3,8192]{1,0:T(4,128)}, f32[64,128]{1,0:T(8,128)}) custom-call(s32[1]{0:T(128)} %get-tuple-element.16.number_ref, s32[8,2560]{1,0:T(8,128)S(1)} %get-tuple-element.17.code_ref, f32[8,8192]{1,0:T(8,128)S(1)} %get-tuple-element.12.own_ref, f32[8,8192]{1,0:T(8,128)S(1)} %get-tuple-element.14.ghost_ref, f32[64,128]{1,0:T(8,128)S(1)} %copy-done.3, ...), custom_call_target="tpu_custom_call" | custom-call | tf_op jit(solution)/shard_map/force/pallas_call | solution.py:353
  (1 shorter events, 0.0 us)
Async XLA Ops:
  0.6 3.1 %copy-start = (f32[8,8192]{1,0:T(8,128)S(1)}, f32[8,8192]{1,0:T(8,128)}, u32[]{:S(2)}) copy-start(f32[8,8192]{1,0:T(8,128)} %particles.1) | copy-start | bytes 786436
  3.7 0.8 copy-start.1
  3.7 0.8 copy-start.4
  56.0 0.7 copy-start.5
  82.9 0.8 copy-start.2
  83.7 10.3 %copy-start.3 = (f32[64,128]{1,0:T(8,128)S(1)}, f32[64,128]{1,0:T(8,128)}, u32[]{:S(2)}) copy-start(f32[64,128]{1,0:T(8,128)} %get-tuple-element.15.density.dens_ref) | copy-start | bytes 98308
where the time goes:
time: 131 us
  Pallas kernels  125 us (95%)
  local copies, waits for them, and re-layouts  2.93 us (2%)
  other arithmetic  1.58 us (1%)
  between operations  1.41 us (1%)
    pallas_call x1, Pallas kernels, exchange(): pl.pallas_call(functools.partial(exchange_kernel, count_x, count_y), name...  51.5 us
    pallas_call x1, Pallas kernels, force_step(): pl.pallas_call(force_kernel, name='force', out_shape=(jax.ShapeDtypeStruc...  36.9 us
    pallas_call x1, Pallas kernels, density_step(): pl.pallas_call(density_kernel, name='density', out_shape=(jax.ShapeDtypeS...  26.3 us
    pallas_call x1, Pallas kernels, ghost_density_step(): pl.pallas_call(functools.partial(ghost_density_kernel, mesh.shape['gx'],...  10.3 us
    unnamed x13, local copies, waits for them, and re-layouts  2.88 us

commit v1 on v0

v1 whole, which is shorter than its diff:
```python
import functools
import math

import jax
import jax.numpy as jnp
from jax import lax
from jax.experimental import pallas as pl
from jax.experimental.pallas import tpu as pltpu
from jax.sharding import PartitionSpec as P

F32 = jnp.float32
BF16 = jnp.bfloat16
I32 = jnp.int32
MASS = 1.0 / 512.0
NEAR = 1e-30
FAR = 1e36
NT_DIMS = (((1,), (1,)), ((), ()))
COLS = 320
STEPS = 384
WAYS = 8
FEW = 4


def iota(shape, axis):
    return lax.broadcasted_iota(I32, shape, axis)


def split3(x):
    a = x.astype(BF16)
    r = x - a.astype(F32)
    b = r.astype(BF16)
    c = (r - b.astype(F32)).astype(BF16)
    return a, b, c


def dot(a, b):
    return jnp.dot(a, b, preferred_element_type=F32)


def dot_nt(a, b):
    return lax.dot_general(a, b, NT_DIMS, preferred_element_type=F32)


def swap_halves(x):
    return pltpu.roll(x, 64, x.ndim - 1)


def ranks_of(active):
    rows, cols = iota((128, 128), 0), iota((128, 128), 1)
    before = ((rows // 64 == cols // 64) & (rows < cols)).astype(F32).astype(BF16)
    rank = dot(active.astype(BF16), before)
    return jnp.where(active > 0.5, rank, -1.0)


def tile_groups(active):
    rows, cols = iota((128, 128), 0), iota((128, 128), 1)
    pick = (rows // 64 == cols % 2).astype(F32).astype(BF16)
    count = dot(active.astype(BF16), pick)
    own = iota((64, 128), 0) == iota((64, 128), 1) // 2
    total = jnp.sum(jnp.where(own, count, 0.0), axis=0, keepdims=True)
    return jnp.floor((total + 7.0) * 0.125)


def item_codes(pairs, used, groups):
    target, source = pairs[0:1], pairs[1:2]
    target_col = pairs.T[:, 0:1]
    count = pairs.shape[1]
    lane = iota((1, count), 1)
    used_row = lane < used
    q, p = iota((count, count), 0), iota((count, count), 1)
    same = (target_col == target) & (q < p) & (q < used)
    order = jnp.sum(jnp.where(same, 1.0, 0.0), axis=0, keepdims=True)
    at = (iota((128, count), 0).astype(F32) == target) & used_row
    at_f = jnp.where(at, 1.0, 0.0)
    number = jnp.sum(at_f, axis=1, keepdims=True)
    columns = jnp.floor((number + 1.0) * 0.5)
    below = (iota((128, 128), 0) > iota((128, 128), 1)).astype(F32).astype(BF16)
    first = dot(below, jnp.broadcast_to(columns, (128, 128)).astype(BF16))[:, 0:1]
    groups_row = dot(groups.astype(BF16), at_f.astype(BF16))
    first_row = jnp.sum(at_f * first, axis=0, keepdims=True)
    half = jnp.floor(order * 0.5)
    column = first_row + half
    second = jnp.where(order - 2.0 * half > 0.5, 1.0, 0.0)
    use = jnp.where(used_row, 1.0, 0.0)
    lead = use * (1.0 - second)
    trail = use * second
    values = jnp.concatenate(
        [target * lead, source * lead, source * trail, trail, groups_row * lead, lead * 0.0, lead * 0.0, lead * 0.0],
        axis=0,
    ).astype(BF16)
    match = jnp.where((iota((COLS, count), 0).astype(F32) == column) & used_row, 1.0, 0.0).astype(BF16)
    in_row = dot_nt(values, match)
    in_col = dot_nt(match, values)
    upper = (iota((COLS, COLS), 0) < iota((COLS, COLS), 1)).astype(F32).astype(BF16)
    lower = (iota((COLS, COLS), 0) > iota((COLS, COLS), 1)).astype(F32).astype(BF16)
    start_row = dot(in_row.astype(BF16), upper)[4:5]
    start_col = dot(lower, in_col.astype(BF16))[:, 4:5]
    size_col = in_col[:, 4:5]
    total = jnp.sum(size_col, axis=0, keepdims=True)
    high = jnp.floor(start_row * (1.0 / 256.0))
    second_source = in_row[2:3] + 256.0 * (1.0 - in_row[3:4])
    table = jnp.concatenate(
        [in_row[0:2], second_source, high, start_row - 256.0 * high, high * 0.0, high * 0.0, high * 0.0], axis=0
    )
    table = jnp.concatenate([table, jnp.zeros((8, 128 * ((COLS + 127) // 128) - COLS), F32)], axis=1)
    before = jnp.where(iota(table.shape, 1) == 0, 0.0, pltpu.roll(table, 1, 1))
    steps = (table - before)[:, 0:COLS].astype(BF16)
    at = iota((1, WAYS * STEPS), 1)
    item = (at % STEPS * WAYS + at // STEPS).astype(F32)
    found = dot(steps, jnp.where(item >= start_col, 1.0, 0.0).astype(BF16))
    beyond = item >= total
    group = item - 256.0 * found[3:4] - found[4:5]
    place = jnp.where(beyond, 0.0, group * 128.0 + found[0:1]).astype(I32)
    first_source = jnp.where(beyond, 256.0, found[1:2]).astype(I32)
    other = jnp.where(beyond, 256.0, found[2:3]).astype(I32)
    codes = place + first_source * 1024 + other * (1 << 19)
    codes = jnp.concatenate([codes[:, STEPS * w : STEPS * w + STEPS] for w in range(WAYS)], axis=0)
    most = jnp.max(groups, axis=1, keepdims=True).astype(I32)
    lane = iota(codes.shape, 1)
    return jnp.where(lane == STEPS - 1, total.astype(I32), jnp.where(lane == STEPS - 2, most, codes))


def put_sources(table, slot, chunk):
    left = iota(chunk.shape, 1) < 64
    other = swap_halves(chunk)
    table[slot] = jnp.where(left, chunk, other)
    table[slot + 1] = jnp.where(left, other, chunk)


def put_targets(columns, tile, chunk, rank, first, last):
    left = iota(chunk.shape, 1) < 64
    a, b, c = [v.astype(F32) for v in split3(chunk)]
    ar, br, cr = swap_halves(a), swap_halves(b), swap_halves(c)
    zero = jnp.zeros_like(a)
    wide = jnp.broadcast_to(rank, (8, 128))
    wide_other = swap_halves(wide)
    left8 = iota((8, 128), 1) < 64
    for half in range(2):
        if half == 0:
            right = jnp.concatenate([jnp.where(left, a, br), jnp.where(left, c, zero)], axis=1)
            own = jnp.where(left8, wide, wide_other)
        else:
            right = jnp.concatenate([jnp.where(left, ar, b), jnp.where(left, cr, zero)], axis=1)
            own = jnp.where(left8, wide_other, wide)
        sub = iota((8, 128), 0).astype(F32)
        pick = jnp.concatenate([jnp.where(own == sub + 8.0 * g, 1.0, 0.0) for g in range(first, last)], axis=0).astype(BF16)
        rows = dot_nt(jnp.concatenate([pick, pick], axis=1), right.astype(BF16))
        for g in range(first, last):
            columns[pl.ds(g * 1024 + (tile + half) * 8, 8), :] = rows[8 * (g - first) : 8 * (g - first) + 8]


def gather_sums(totals, tile, rank, first, last):
    left = iota((8, 128), 1) < 64
    wide = jnp.broadcast_to(rank, (8, 128))
    sub = iota((8, 128), 0).astype(F32)
    out = [jnp.zeros((8, 128), F32) for _ in totals]
    for g in range(first, last):
        hit = wide == sub + 8.0 * g
        for n, total in enumerate(totals):
            one = jnp.sum(total[pl.ds(g * 1024 + tile * 8, 8), :], axis=1, keepdims=True)
            two = jnp.sum(total[pl.ds(g * 1024 + tile * 8 + 8, 8), :], axis=1, keepdims=True)
            out[n] = out[n] + jnp.where(hit, jnp.where(left, one, two), 0.0)
    return [jnp.sum(o, axis=0, keepdims=True) for o in out]


def wrapped(a, b):
    s = a - b
    return s - jnp.floor(s + 0.5)


def decode(code):
    return code & 1023, (code >> 10) & 511, code >> 19


def density_item(code, columns, sources):
    place, one, two = decode(code)
    row = pl.multiple_of(place * 8, 8)
    mine = columns[pl.ds(row, 8), :]
    left = iota((8, 128), 1) < 64
    other = jnp.where(left, sources[one], sources[two])
    dx = wrapped(mine[:, 0:1], other[0:1])
    dy = wrapped(mine[:, 1:2], other[1:2])
    dz = wrapped(mine[:, 2:3], other[2:3])
    rsq = jnp.maximum(dx * dx + dy * dy + dz * dz, other[3:4])
    q = rsq * lax.rsqrt(rsq) * mine[:, 3:4]
    t = jnp.maximum(2.0 - q, 0.0)
    u = jnp.maximum(1.0 - q, 0.0)
    w = t * t * t - 4.0 * (u * u * u)
    return row, w


def force_item(code, columns, sources):
    place, one, two = decode(code)
    row = pl.multiple_of(place * 8, 8)
    mine = columns[pl.ds(row, 8), :]
    left = iota((16, 128), 1) < 64
    other = jnp.where(left, sources[one], sources[two])
    dx = wrapped(mine[:, 0:1], other[0:1])
    dy = wrapped(mine[:, 1:2], other[1:2])
    dz = wrapped(mine[:, 2:3], other[2:3])
    rsq = jnp.maximum(dx * dx + dy * dy + dz * dz, other[10:11])
    inv = lax.rsqrt(rsq)
    r = rsq * inv

    def profile(h, hinv):
        q = r * hinv
        t = jnp.maximum(2.0 - q, 0.0)
        return jnp.where(q < 1.0, 4.0 - 3.0 * q, t * t * (h * inv))

    slope = profile(mine[:, 6:7], mine[:, 8:9]) * mine[:, 9:10] + profile(other[6:7], other[8:9]) * other[9:10]
    w = (mine[:, 7:8] + other[7:8]) * slope
    gap = (
        (mine[:, 3:4] - other[3:4]) * dx
        + (mine[:, 4:5] - other[4:5]) * dy
        + (mine[:, 5:6] - other[5:6]) * dz
    )
    return row, (w * dx, w * dy, w * dz, w * gap)


def for_all_groups(most, body):
    body(0, FEW, False)

    @pl.when(most > FEW)
    def _():
        body(FEW, 8, True)


def run_items(number, codes, item):
    @pl.loop(0, (number + 2 * WAYS - 1) // (2 * WAYS))
    def _(pair):
        for late in range(2):
            for way in range(WAYS):
                item(codes[way, 2 * pair + late])


def density_kernel(count_ref, pairs_ref, own_ref, extra_ref, ghost_ref, dens_ref, code_ref, rank_ref,
                   sources, columns, total, sums, smooth, codes_s, sem):
    active = extra_ref[pl.ds(1, 64, stride=2), :]
    rank_ref[...] = ranks_of(active)
    pairs = jnp.concatenate([pairs_ref[...].astype(F32), jnp.zeros((6, 512), F32)], axis=0)
    code_ref[...] = item_codes(pairs, count_ref[0], tile_groups(active))
    copy = pltpu.make_async_copy(code_ref, codes_s, sem)
    copy.start()

    def fields(block):
        sub = iota((8, 128), 0)
        return jnp.where(sub < 3, block, jnp.where(sub == 3, NEAR, 0.0))

    def targets(block):
        sub = iota((8, 128), 0)
        return jnp.where(sub < 3, block, jnp.where(sub == 3, 1.0 / block[6:7], 0.0))

    @pl.loop(0, 16)
    def _(step):
        for part in range(4):
            chunk = step * 4 + part
            lanes = pl.ds(pl.multiple_of(step * 512, 512) + 128 * part, 128)
            block = own_ref[:, lanes]
            smooth[pl.ds(chunk, 1), :] = block[6:7]
            put_sources(sources, chunk * 2, fields(block))
            put_sources(sources, chunk * 2 + 128, fields(ghost_ref[:, lanes]))

    sources[256] = jnp.where(iota((8, 128), 0) == 3, FAR, 0.0)
    copy.wait()
    number, most = codes_s[0, STEPS - 1], codes_s[0, STEPS - 2]

    def prepare(first, last, again):
        @pl.loop(0, 16)
        def _(step):
            for part in range(4):
                chunk = step * 4 + part
                lanes = pl.ds(pl.multiple_of(step * 512, 512) + 128 * part, 128)
                put_targets(columns, chunk * 2, targets(own_ref[:, lanes]), rank_ref[pl.ds(chunk, 1), :], first, last)
                for g in range(first, last):
                    total[pl.ds(g * 1024 + chunk * 16, 16), :] = jnp.zeros((16, 128), F32)

    for_all_groups(most, prepare)

    def item(code):
        row, w = density_item(code, columns, sources)
        total[pl.ds(row, 8), :] += w

    run_items(number, codes_s, item)

    def collect(first, last, again):
        @pl.loop(0, 16)
        def _(step):
            for part in range(4):
                chunk = step * 4 + part
                (got,) = gather_sums([total], chunk * 2, rank_ref[pl.ds(chunk, 1), :], first, last)
                at = pl.ds(chunk, 1)
                sums[at, :] = sums[at, :] + got if again else got

    for_all_groups(most, collect)
    h = smooth[...]
    fresh = MASS / math.pi / (h * h * h) * (1.0 + 0.25 * sums[...])
    dens_ref[...] = jnp.where(rank_ref[...] >= 0.0, fresh, extra_ref[pl.ds(0, 64, stride=2), :])


def force_kernel(code_ref, own_ref, ghost_ref, dens_ref, gdens_ref, rank_ref, acc_ref, heat_ref,
                 sources, columns, ax, ay, az, heat):
    number, most = code_ref[0, STEPS - 1], code_ref[0, STEPS - 2]

    def fields(block, density):
        h = block[6:7]
        press = (5.0 / 3.0 - 1.0) * block[7:8] / density
        hinv = 1.0 / h
        scale = (0.375 * MASS / math.pi) / (h * h * h * h * h)
        near = jnp.full((1, 128), NEAR, F32)
        return jnp.concatenate([block[0:7], press, hinv, scale, near, jnp.zeros((5, 128), F32)], axis=0)

    def own_fields(step, part):
        lanes = pl.ds(pl.multiple_of(step * 512, 512) + 128 * part, 128)
        return fields(own_ref[:, lanes], dens_ref[pl.ds(step * 4 + part, 1), :])

    @pl.loop(0, 16)
    def _(step):
        for part in range(4):
            chunk = step * 4 + part
            lanes = pl.ds(pl.multiple_of(step * 512, 512) + 128 * part, 128)
            put_sources(sources, chunk * 2, own_fields(step, part))
            put_sources(sources, chunk * 2 + 128, fields(ghost_ref[:, lanes], gdens_ref[pl.ds(chunk, 1), :]))

    def prepare(first, last, again):
        @pl.loop(0, 16)
        def _(step):
            for part in range(4):
                chunk = step * 4 + part
                put_targets(columns, chunk * 2, own_fields(step, part), rank_ref[pl.ds(chunk, 1), :], first, last)
                for g in range(first, last):
                    for total in (ax, ay, az, heat):
                        total[pl.ds(g * 1024 + chunk * 16, 16), :] = jnp.zeros((16, 128), F32)

    for_all_groups(most, prepare)
    sub = iota((16, 128), 0)
    sources[256] = jnp.where(sub == 10, FAR, jnp.where((sub == 6) | (sub == 8), 1.0, 0.0))

    def item(code):
        row, terms = force_item(code, columns, sources)
        for total, term in zip((ax, ay, az, heat), terms):
            total[pl.ds(row, 8), :] += term

    run_items(number, code_ref, item)

    def collect(first, last, again):
        @pl.loop(0, 16)
        def _(step):
            for part in range(4):
                chunk = step * 4 + part
                got = gather_sums([ax, ay, az, heat], chunk * 2, rank_ref[pl.ds(chunk, 1), :], first, last)
                lanes = pl.ds(pl.multiple_of(step * 512, 512) + 128 * part, 128)
                at = pl.ds(chunk, 1)
                for n in range(3):
                    acc_ref[n : n + 1, lanes] = acc_ref[n : n + 1, lanes] + got[n] if again else got[n]
                heat_ref[at, :] = heat_ref[at, :] - 0.5 * got[3] if again else -0.5 * got[3]

    for_all_groups(most, collect)


VM = pl.BlockSpec(memory_space=pltpu.VMEM)
SM = pl.BlockSpec(memory_space=pltpu.SMEM)


def density_step(pair_count, pair_tiles, own, extra, ghost):
    return pl.pallas_call(
        density_kernel,
        name="density",
        out_shape=(
            jax.ShapeDtypeStruct((64, 128), F32),
            jax.ShapeDtypeStruct((WAYS, STEPS), I32),
            jax.ShapeDtypeStruct((64, 128), F32),
        ),
        in_specs=[SM, VM, VM, VM, VM],
        out_specs=(VM, VM, VM),
        scratch_shapes=[
            pltpu.VMEM((257, 8, 128), F32),
            pltpu.VMEM((8192, 8), F32),
            pltpu.VMEM((8192, 128), F32),
            pltpu.VMEM((64, 128), F32),
            pltpu.VMEM((64, 128), F32),
            pltpu.SMEM((WAYS, STEPS), I32),
            pltpu.SemaphoreType.DMA,
        ],
        compiler_params=pltpu.CompilerParams(vmem_limit_bytes=48 << 20),
    )(pair_count, pair_tiles, own, extra, ghost)


def force_step(codes, own, ghost, density, ghost_density, rank):
    return pl.pallas_call(
        force_kernel,
        name="force",
        out_shape=(jax.ShapeDtypeStruct((3, 8192), F32), jax.ShapeDtypeStruct((64, 128), F32)),
        in_specs=[SM, VM, VM, VM, VM, VM],
        out_specs=(VM, VM),
        scratch_shapes=[pltpu.VMEM((257, 16, 128), F32), pltpu.VMEM((8192, 16), F32)]
        + [pltpu.VMEM((8192, 128), F32)] * 4,
        compiler_params=pltpu.CompilerParams(vmem_limit_bytes=48 << 20),
    )(codes, own, ghost, density, ghost_density, rank)


LEVELS = 4
SEND = 2048
PIECE = 512
PIECES = SEND // PIECE
GHOSTS = 1024
MESH = pl.DeviceIdType.MESH


def flipped(index, bit):
    step = 1 << bit
    return index + step - 2 * step * ((index // step) % 2)


def neighbour(number, sign, count_x, count_y):
    cell = number + number // 4
    i = (lax.axis_index("gx") + sign * (cell // 3 - 1) + count_x) % count_x
    j = (lax.axis_index("gy") + sign * (cell % 3 - 1) + count_y) % count_y
    return i, j


def permuted(value, lanes):
    return jnp.take_along_axis(value, lanes, axis=1, mode="promise_in_bounds")


def one_hot(index_row):
    low = jnp.bitwise_and(index_row, 255)
    return jnp.where(iota((256, index_row.shape[1]), 0) == low, 1.0, 0.0).astype(BF16)


def chosen(read, bits, first, count):
    if count == 1:
        return read(first)
    half = count // 2
    low = chosen(read, bits, first, half)
    high = chosen(read, bits, first + half, half)
    return jnp.where(bits[half.bit_length() - 1], high, low)


def digits_of(value, count):
    return [jnp.bitwise_and(value, 1 << n) != 0 for n in range(count)]


def rows_at(state, index):
    index = jnp.broadcast_to(index, (8, 128))
    low = jnp.bitwise_and(index, 127)
    return chosen(lambda c: permuted(state[:, 128 * c : 128 * c + 128], low), digits_of(index >> 7, 6), 0, 64)


def pairs_at(extra, index, groups):
    index = jnp.broadcast_to(index, (8, 128))
    low = jnp.bitwise_and(index, 127)
    bits = digits_of(index >> 9, groups.bit_length() - 1)
    out = chosen(lambda g: permuted(extra[8 * g : 8 * g + 8, :], low), bits, 0, groups)
    out = jnp.where(iota((8, 128), 0) >> 1 == jnp.bitwise_and(index >> 7, 3), out, 0.0)
    out = out + pltpu.roll(out, 4, 0)
    return out + pltpu.roll(out, 2, 0)


def cells_at(table, index):
    index = jnp.broadcast_to(index, (8, 128))
    low, high = jnp.bitwise_and(index, 127), (index >> 7) - iota((8, 128), 0)
    out = jnp.zeros((8, 128), table.dtype)
    for v in range(8):
        out = jnp.where(high == 8 * v, permuted(table[8 * v : 8 * v + 8, :], low), out)
    return jnp.sum(out, axis=0, keepdims=True)


def landed(read, slot, old):
    low = jnp.bitwise_and(slot, 127)
    new = chosen(lambda c: permuted(read(c), low), digits_of(slot >> 7, 4), 0, 16)
    return jnp.where(slot >= 0, new, old)


def exchange_kernel(count_x, count_y, counts, particles, extra_in, rows, exports, own, extra, ghost,
                    hot, inverse, inverse_wide, slots, slots_x, exports_3, base_main, base_extra,
                    send_main, send_extra, recv_main, recv_extra, recv_wide,
                    send_ghost, send_sems, recv_sems, ghost_send, ghost_recv):
    i, j = lax.axis_index("gx"), lax.axis_index("gy")
    bits_x, bits_y = count_x.bit_length() - 1, count_y.bit_length() - 1
    partners = [
        (flipped(i, bits_x - 1), j),
        (flipped(i, bits_x - 2), j),
        (i, flipped(j, bits_y - 1)),
        (i, flipped(j, bits_y - 2)),
    ]
    barrier = pltpu.get_barrier_semaphore()
    for partner in partners:
        pl.semaphore_signal(barrier, inc=1, device_id=partner, device_id_type=MESH)
    for number in range(8):
        pl.semaphore_signal(barrier, inc=1, device_id=neighbour(number, 1, count_x, count_y), device_id_type=MESH)

    def invert(level):
        slot = iota((32, SEND), 1)
        index = rows[level : level + 1, :]
        high = jnp.where(slot < counts[level, 0], jnp.broadcast_to(index >> 8, (32, SEND)), 64)
        here = iota((32, SEND), 0) == high
        digits = jnp.concatenate(
            [
                jnp.where(here, ((slot >> 7) + 1).astype(F32), 0.0),
                jnp.where(here, jnp.bitwise_and(slot, 127).astype(F32), 0.0),
            ],
            axis=0,
        ).astype(BF16)
        for piece in range(PIECES):
            hot[:, piece * PIECE : piece * PIECE + PIECE] = one_hot(index[:, piece * PIECE : piece * PIECE + PIECE])
        found = dot_nt(digits, hot[...])
        found = (128.0 * (found[0:32] - 1.0) + found[32:64]).astype(I32)
        for part in range(2):
            value = found[:, 128 * part : 128 * part + 128]
            inverse[pl.ds(part, 32, stride=2), :] = value
            for field in range(2):
                inverse_wide[level, pl.ds(2 * part + field, 32, stride=4), :] = value

    def main_copy(level, piece):
        lanes = pl.ds(pl.multiple_of(piece * PIECE, PIECE), PIECE)
        return pltpu.make_async_remote_copy(
            src_ref=send_main.at[level, :, lanes],
            dst_ref=recv_main.at[level, :, lanes],
            send_sem=send_sems.at[level, piece],
            recv_sem=recv_sems.at[level, piece],
            device_id=partners[level],
            device_id_type=MESH,
        )

    def extra_copy(level):
        return pltpu.make_async_remote_copy(
            src_ref=send_extra.at[level],
            dst_ref=recv_extra.at[level],
            send_sem=send_sems.at[level, PIECES],
            recv_sem=recv_sems.at[level, PIECES],
            device_id=partners[level],
            device_id_type=MESH,
        )

    def ghost_copy(number):
        lanes = pl.ds(pl.multiple_of(number * GHOSTS, GHOSTS), GHOSTS)
        return pltpu.make_async_remote_copy(
            src_ref=send_ghost.at[:, lanes],
            dst_ref=ghost.at[:, lanes],
            send_sem=ghost_send.at[number],
            recv_sem=ghost_recv.at[number],
            device_id=neighbour(number, 1, count_x, count_y),
            device_id_type=MESH,
        )

    def gather(level, out):
        @pl.loop(0, PIECES)
        def _(piece):
            for k in range(PIECE // 128):
                at = pl.multiple_of(piece * PIECE + 128 * k, 128)
                index = rows[level : level + 1, pl.ds(at, 128)]
                out[:, pl.ds(at, 128)] = rows_at(own, index)
                base_extra[:, pl.ds(at, 128)] = pairs_at(extra, index, 16)

    def compose(level):
        @pl.loop(0, PIECES)
        def _(piece):
            for k in range(PIECE // 128):
                at = pl.multiple_of(piece * PIECE + 128 * k, 128)
                slots[:, pl.ds(at, 128)] = cells_at(inverse, rows[level : level + 1, pl.ds(at, 128)])

    def send(level):
        for piece in range(PIECES):
            for k in range(PIECE // 128):
                c = piece * (PIECE // 128) + k
                lanes = slice(128 * c, 128 * c + 128)
                both = base_extra[:, lanes]
                if level > 0:
                    slot = jnp.broadcast_to(slots[:, lanes], (8, 128))
                    send_main[level, :, lanes] = landed(
                        lambda n: recv_main[level - 1, :, 128 * n : 128 * n + 128], slot, base_main[:, lanes]
                    )
                    fresh = pairs_at(recv_extra.at[level - 1], jnp.maximum(slots[:, lanes], 0), 4)
                    both = jnp.where(slot >= 0, fresh, both)
                send_extra[level, 2 * c : 2 * c + 2, :] = both[0:2]
            main_copy(level, piece).start()
        extra_copy(level).start()

    def arrive(level):
        extra_copy(level).wait()
        for piece in range(PIECES):
            main_copy(level, piece).wait()

    def settle(level):
        for c in range(16):
            wide = jnp.concatenate([recv_extra[level, 2 * c : 2 * c + 2, :]] * 4, axis=0)
            recv_wide[:, 128 * c : 128 * c + 128] = wide

        @pl.loop(0, 16)
        def _(g):
            at = pl.multiple_of(g * 8, 8)
            slot = inverse_wide[level, pl.ds(at, 8), :]
            extra[pl.ds(at, 8), :] = landed(lambda c: recv_wide[:, 128 * c : 128 * c + 128], slot, extra[pl.ds(at, 8), :])
            for b in range(4):
                lanes = pl.ds(pl.multiple_of(g * 512, 512) + 128 * b, 128)
                slot_b = jnp.broadcast_to(slot[2 * b : 2 * b + 1], (8, 128))
                own[:, lanes] = landed(
                    lambda c: recv_main[level, :, 128 * c : 128 * c + 128], slot_b, own[:, lanes]
                )

    own[...] = particles[...]
    extra[...] = extra_in[...]
    for number in range(8):
        exports_3[number] = exports[number : number + 1, :]
    gather(0, send_main.at[0])
    pl.semaphore_wait(barrier, 12)

    for level in range(LEVELS):
        send(level)
        invert(level)
        if level > 0:
            settle(level - 1)
        if level + 1 < LEVELS:
            compose(level + 1)
            gather(level + 1, base_main)
        else:

            @pl.loop(0, 16)
            def _(block):
                number, part = block // 2, block % 2
                for k in range(4):
                    lanes = pl.multiple_of(part * 512 + 128 * k, 128)
                    index = exports_3[number, :, pl.ds(lanes, 128)]
                    slots_x[number, :, pl.ds(lanes, 128)] = cells_at(inverse, index)
                    send_ghost[:, pl.ds(pl.multiple_of(number * GHOSTS + lanes, 128), 128)] = rows_at(own, index)

        arrive(level)

    @pl.loop(0, 8)
    def _(number):
        for k in range(8):
            lanes = pl.ds(pl.multiple_of(number * GHOSTS, GHOSTS) + 128 * k, 128)
            slot = jnp.broadcast_to(slots_x[number, :, 128 * k : 128 * k + 128], (8, 128))
            send_ghost[:, lanes] = landed(
                lambda n: recv_main[LEVELS - 1, :, 128 * n : 128 * n + 128], slot, send_ghost[:, lanes]
            )
        ghost_copy(number).start()

    settle(LEVELS - 1)
    for number in range(8):
        ghost_copy(number).wait()


def exchange(mesh, send_count, particles, extra, send_rows, export_rows):
    count_x, count_y = mesh.shape["gx"], mesh.shape["gy"]
    return pl.pallas_call(
        functools.partial(exchange_kernel, count_x, count_y),
        name="exchange",
        out_shape=(
            jax.ShapeDtypeStruct((8, 8192), F32),
            jax.ShapeDtypeStruct((128, 128), F32),
            jax.ShapeDtypeStruct((8, 8192), F32),
        ),
        in_specs=[SM, VM, VM, VM, VM],
        out_specs=(VM, VM, VM),
        scratch_shapes=[
            pltpu.VMEM((256, SEND), BF16),
            pltpu.VMEM((64, 128), I32),
            pltpu.VMEM((LEVELS, 128, 128), I32),
            pltpu.VMEM((1, SEND), I32),
            pltpu.VMEM((8, 1, GHOSTS), I32),
            pltpu.VMEM((8, 1, GHOSTS), I32),
            pltpu.VMEM((8, SEND), F32),
            pltpu.VMEM((8, SEND), F32),
            pltpu.VMEM((LEVELS, 8, SEND), F32),
            pltpu.VMEM((LEVELS, 32, 128), F32),
            pltpu.VMEM((LEVELS, 8, SEND), F32),
            pltpu.VMEM((LEVELS, 32, 128), F32),
            pltpu.VMEM((8, SEND), F32),
            pltpu.VMEM((8, 8 * GHOSTS), F32),
            pltpu.SemaphoreType.DMA((LEVELS, PIECES + 1)),
            pltpu.SemaphoreType.DMA((LEVELS, PIECES + 1)),
            pltpu.SemaphoreType.DMA((8,)),
            pltpu.SemaphoreType.DMA((8,)),
        ],
        compiler_params=pltpu.CompilerParams(
            collective_id=0, has_side_effects=True, vmem_limit_bytes=48 << 20
        ),
    )(send_count, particles, extra, send_rows, export_rows)


def ghost_density_kernel(count_x, count_y, density, exports, out, exports_3, send, send_sems, recv_sems):
    barrier = pltpu.get_barrier_semaphore()
    for number in range(8):
        pl.semaphore_signal(barrier, inc=1, device_id=neighbour(number, 1, count_x, count_y), device_id_type=MESH)
    for number in range(8):
        exports_3[number] = exports[number : number + 1, :]
    def copy(number):
        return pltpu.make_async_remote_copy(
            src_ref=send.at[number],
            dst_ref=out.at[number],
            send_sem=send_sems.at[number],
            recv_sem=recv_sems.at[number],
            device_id=neighbour(number, 1, count_x, count_y),
            device_id_type=MESH,
        )

    def gathered(number):
        for k in range(8):
            send[number, k : k + 1, :] = cells_at(density, exports_3[number, :, 128 * k : 128 * k + 128])

    gathered(0)
    pl.semaphore_wait(barrier, 8)
    copy(0).start()

    @pl.loop(1, 8)
    def _(number):
        gathered(number)
        copy(number).start()

    for number in range(8):
        copy(number).wait()


def ghost_density_step(mesh, density, export_rows):
    return pl.pallas_call(
        functools.partial(ghost_density_kernel, mesh.shape["gx"], mesh.shape["gy"]),
        name="ghost_density",
        out_shape=jax.ShapeDtypeStruct((8, 8, 128), F32),
        in_specs=[VM, VM],
        out_specs=VM,
        scratch_shapes=[
            pltpu.VMEM((8, 1, GHOSTS), I32),
            pltpu.VMEM((8, 8, 128), F32),
            pltpu.SemaphoreType.DMA((8,)),
            pltpu.SemaphoreType.DMA((8,)),
        ],
        compiler_params=pltpu.CompilerParams(collective_id=1, has_side_effects=True, vmem_limit_bytes=32 << 20),
    )(density, export_rows)


def on_device(
    mesh, particles, old_density, active, send_rows, send_count, export_rows, pair_tiles, pair_count
):
    extra = jnp.stack([old_density.reshape(64, 128), active.astype(F32).reshape(64, 128)], axis=1).reshape(128, 128)
    own, extra, ghost = exchange(mesh, send_count, particles, extra, send_rows, export_rows)
    density, codes, rank = density_step(pair_count, pair_tiles, own, extra, ghost)
    ghost_density = ghost_density_step(mesh, density, export_rows).reshape(64, 128)
    acceleration, heating = force_step(codes, own, ghost, density, ghost_density, rank)
    return density.reshape(8192), acceleration, heating.reshape(8192)


def solution(mesh):
    in_specs = (
        P(None, ("gx", "gy")),
        P(("gx", "gy")),
        P(("gx", "gy")),
        P(None, ("gx", "gy")),
        P(None, ("gx", "gy")),
        P(None, ("gx", "gy")),
        P(None, ("gx", "gy")),
        P(("gx", "gy")),
    )
    out_specs = (P(("gx", "gy")), P(None, ("gx", "gy")), P(("gx", "gy")))
    return jax.shard_map(
        functools.partial(on_device, mesh), mesh=mesh, in_specs=in_specs, out_specs=out_specs, check_vma=False
    )
```

time: 131 us -> 107 us (0.82)
  Pallas kernels: 125 us -> 100 us
    pallas_call x1, Pallas kernels: 36.9 us -> 26.7 us  [force_step(): pl.pallas_call(force_kernel, name='force', out_shape=(jax.ShapeDtypeStruc...]
    pallas_call x1, Pallas kernels: 26.3 us -> 18.2 us  [density_step(): pl.pallas_call(density_kernel, name='density', out_shape=(jax.ShapeDtypeS...]
    pallas_call x1, Pallas kernels: 51.5 us -> 45.3 us  [exchange(): pl.pallas_call(functools.partial(exchange_kernel, count_x, count_y), name...]
    unnamed x13 -> x17, local copies, waits for them, and re-layouts: 2.88 us -> 3.83 us
where the time goes in v1:
time: 107 us; the launch traced here: 106 us
  Pallas kernels  100 us (93%)
  local copies, waits for them, and re-layouts  3.83 us (4%)
  between operations  1.35 us (1%)
    pallas_call x1, Pallas kernels, exchange(): pl.pallas_call(functools.partial(exchange_kernel, count_x, count_y), name...  45.3 us
    pallas_call x1, Pallas kernels, force_step(): pl.pallas_call(force_kernel, name='force', out_shape=(jax.ShapeDtypeStruc...  26.7 us
    pallas_call x1, Pallas kernels, density_step(): pl.pallas_call(density_kernel, name='density', out_shape=(jax.ShapeDtypeS...  18.2 us
    pallas_call x1, Pallas kernels, ghost_density_step(): pl.pallas_call(functools.partial(ghost_density_kernel, mesh.shape['gx'],...  9.95 us
    unnamed x17, local copies, waits for them, and re-layouts  3.83 us

profile of v1, /device:TPU:0, one launch (start us, length us, event | category | flops | bytes accessed | tf_op | source)
XLA Modules:
  0.0 106.2 jit_solution(6361706276047403520)
XLA Ops:
  1.3 0.0 copy-start.7
  1.3 0.6 copy-done.7
  1.9 0.1 copy.11.counts
  2.0 0.0 copy-start.6
  2.0 0.8 convert_element_type.3
  2.8 0.0 copy-done.6
  2.8 0.0 copy-start.1
  2.8 0.0 copy-start.4
  2.8 0.1 pad_maximum_fusion
  2.9 0.7 copy-done.1
  3.6 0.0 copy-done.4
  3.6 0.0 copy-start
  3.6 0.9 copy-done
  4.5 45.3 %exchange.1 = (f32[8,8192]{1,0:T(8,128)S(1)}, f32[128,128]{1,0:T(8,128)S(1)}, f32[8,8192]{1,0:T(8,128)S(1)}) custom-call(s32[4,1]{1,0:T(4,128)S(1)} %copy.11.counts, f32[8,8192]{1,0:T(8,128)S(1)} %copy-done, f32[128,128]{1,0:T(8,128)S(1)} %bitcast.6, s32[4,2048]{1,0:T(4,128)S(1)} %copy-done.4, s32[8,1024]{1,0:T(8,128)S(1)} %copy-done.1), custom_call_target="tpu_custom_call" | custom-call | tf_op jit(solution)/shard_map/exchange/pallas_call | solution.py:646
  49.8 0.0 copy-start.5
  49.9 0.7 copy-done.5
  50.5 18.2 %density.1 = (f32[64,128]{1,0:T(8,128)}, s32[8,384]{1,0:T(8,128)S(1)}, f32[64,128]{1,0:T(8,128)S(1)}) custom-call(s32[1]{0:T(128)S(6)} %copy.12.count_ref, s32[2,512]{1,0:T(2,128)S(1)} %copy-done.5, f32[8,8192]{1,0:T(8,128)S(1)} %get-tuple-element.11.own_ref, f32[128,128]{1,0:T(8,128)S(1)} %get-tuple-element.12.extra_ref, ...), custom_call_target="tpu_custom_call" | custom-call | tf_op jit(solution)/shard_map/density/pallas_call | solution.py:365
  68.7 0.0 copy-start.2
  68.7 0.7 copy-done.2
  69.5 0.0 copy-start.3
  69.5 10.0 %ghost_density.1 = f32[8,8,128]{2,1,0:T(8,128)S(1)} custom-call(f32[64,128]{1,0:T(8,128)S(1)} %copy-done.2, s32[8,1024]{1,0:T(8,128)S(1)} %copy-done.1), custom_call_target="tpu_custom_call" | custom-call | tf_op jit(solution)/shard_map/ghost_density/pallas_call | solution.py:716
  79.5 0.0 copy-done.3
  79.5 26.7 %force.1 = (f32[3,8192]{1,0:T(4,128)}, f32[64,128]{1,0:T(8,128)}) custom-call(s32[8,384]{1,0:T(8,128)S(1)} %get-tuple-element.15.code_ref, f32[8,8192]{1,0:T(8,128)S(1)} %get-tuple-element.11.own_ref, f32[8,8192]{1,0:T(8,128)S(1)} %get-tuple-element.13.ghost_ref, f32[64,128]{1,0:T(8,128)S(1)} %copy-done.3, f32[64,128]{1,0:T(8,128)S(1)} %bitcast.8, ...), custom_call_target="tpu_custom_call" | custom-call | tf_op jit(solution)/shard_map/force/pallas_call | solution.py:389
Async XLA Ops:
  1.3 0.7 copy-start.7
  2.0 0.8 copy-start.6
  2.8 0.8 copy-start.1
  2.8 0.8 copy-start.4
  3.6 0.9 copy-start
  49.8 0.7 copy-start.5
  68.7 0.8 copy-start.2
  69.5 10.0 %copy-start.3 = (f32[64,128]{1,0:T(8,128)S(1)}, f32[64,128]{1,0:T(8,128)}, u32[]{:S(2)}) copy-start(f32[64,128]{1,0:T(8,128)} %get-tuple-element.14.density.dens_ref) | copy-start | bytes 98308

commit v2 on v1

--- a/solution.py
+++ b/solution.py
@@ -61,12 +61,11 @@
     return jnp.floor((total + 7.0) * 0.125)
 
 
-def item_codes(pairs, used, groups):
+def pair_columns(pairs, used):
     target, source = pairs[0:1], pairs[1:2]
-    target_col = pairs.T[:, 0:1]
     count = pairs.shape[1]
-    lane = iota((1, count), 1)
-    used_row = lane < used
+    target_col = jnp.broadcast_to(target, (8, count)).T[:, 0:1]
+    used_row = iota((1, count), 1) < used
     q, p = iota((count, count), 0), iota((count, count), 1)
     same = (target_col == target) & (q < p) & (q < used)
     order = jnp.sum(jnp.where(same, 1.0, 0.0), axis=0, keepdims=True)
@@ -76,7 +75,6 @@
     columns = jnp.floor((number + 1.0) * 0.5)
     below = (iota((128, 128), 0) > iota((128, 128), 1)).astype(F32).astype(BF16)
     first = dot(below, jnp.broadcast_to(columns, (128, 128)).astype(BF16))[:, 0:1]
-    groups_row = dot(groups.astype(BF16), at_f.astype(BF16))
     first_row = jnp.sum(at_f * first, axis=0, keepdims=True)
     half = jnp.floor(order * 0.5)
     column = first_row + half
@@ -84,23 +82,27 @@
     use = jnp.where(used_row, 1.0, 0.0)
     lead = use * (1.0 - second)
     trail = use * second
+    zero = lead * 0.0
     values = jnp.concatenate(
-        [target * lead, source * lead, source * trail, trail, groups_row * lead, lead * 0.0, lead * 0.0, lead * 0.0],
-        axis=0,
+        [target * lead, source * lead, source * trail, lead, trail, zero, zero, zero], axis=0
     ).astype(BF16)
     match = jnp.where((iota((COLS, count), 0).astype(F32) == column) & used_row, 1.0, 0.0).astype(BF16)
-    in_row = dot_nt(values, match)
-    in_col = dot_nt(match, values)
+    found = dot_nt(values, match)
+    alone = 256.0 * (1.0 - found[4:5])
+    return jnp.where(iota(found.shape, 0) == 2, found + alone, found)
+
+
+def item_codes(in_row, groups):
+    tile = jnp.where(iota((128, COLS), 0).astype(F32) == in_row[0:1], 1.0, 0.0).astype(BF16)
+    size = dot(jnp.broadcast_to(groups, (8, 128)).astype(BF16), tile) * in_row[3:4]
     upper = (iota((COLS, COLS), 0) < iota((COLS, COLS), 1)).astype(F32).astype(BF16)
     lower = (iota((COLS, COLS), 0) > iota((COLS, COLS), 1)).astype(F32).astype(BF16)
-    start_row = dot(in_row.astype(BF16), upper)[4:5]
-    start_col = dot(lower, in_col.astype(BF16))[:, 4:5]
-    size_col = in_col[:, 4:5]
-    total = jnp.sum(size_col, axis=0, keepdims=True)
+    start_row = dot(size.astype(BF16), upper)[0:1]
+    start_col = dot_nt(lower, size.astype(BF16))[:, 0:1]
+    total = jnp.sum(size[0:1], axis=1, keepdims=True)
     high = jnp.floor(start_row * (1.0 / 256.0))
-    second_source = in_row[2:3] + 256.0 * (1.0 - in_row[3:4])
     table = jnp.concatenate(
-        [in_row[0:2], second_source, high, start_row - 256.0 * high, high * 0.0, high * 0.0, high * 0.0], axis=0
+        [in_row[0:3], high, start_row - 256.0 * high, high * 0.0, high * 0.0, high * 0.0], axis=0
     )
     table = jnp.concatenate([table, jnp.zeros((8, 128 * ((COLS + 127) // 128) - COLS), F32)], axis=1)
     before = jnp.where(iota(table.shape, 1) == 0, 0.0, pltpu.roll(table, 1, 1))
@@ -233,12 +235,11 @@
                 item(codes[way, 2 * pair + late])
 
 
-def density_kernel(count_ref, pairs_ref, own_ref, extra_ref, ghost_ref, dens_ref, code_ref, rank_ref,
+def density_kernel(cols_ref, own_ref, extra_ref, ghost_ref, result_ref, dens_ref, code_ref, rank_ref,
                    sources, columns, total, sums, smooth, codes_s, sem):
     active = extra_ref[pl.ds(1, 64, stride=2), :]
     rank_ref[...] = ranks_of(active)
-    pairs = jnp.concatenate([pairs_ref[...].astype(F32), jnp.zeros((6, 512), F32)], axis=0)
-    code_ref[...] = item_codes(pairs, count_ref[0], tile_groups(active))
+    code_ref[...] = item_codes(cols_ref[...], tile_groups(active))
     copy = pltpu.make_async_copy(code_ref, codes_s, sem)
     copy.start()
 
@@ -294,7 +295,9 @@
     for_all_groups(most, collect)
     h = smooth[...]
     fresh = MASS / math.pi / (h * h * h) * (1.0 + 0.25 * sums[...])
-    dens_ref[...] = jnp.where(rank_ref[...] >= 0.0, fresh, extra_ref[pl.ds(0, 64, stride=2), :])
+    fresh = jnp.where(rank_ref[...] >= 0.0, fresh, extra_ref[pl.ds(0, 64, stride=2), :])
+    dens_ref[...] = fresh
+    result_ref[...] = fresh
 
 
 def force_kernel(code_ref, own_ref, ghost_ref, dens_ref, gdens_ref, rank_ref, acc_ref, heat_ref,
@@ -361,17 +364,18 @@
 SM = pl.BlockSpec(memory_space=pltpu.SMEM)
 
 
-def density_step(pair_count, pair_tiles, own, extra, ghost):
+def density_step(columns, own, extra, ghost):
     return pl.pallas_call(
         density_kernel,
         name="density",
         out_shape=(
             jax.ShapeDtypeStruct((64, 128), F32),
+            jax.ShapeDtypeStruct((64, 128), F32),
             jax.ShapeDtypeStruct((WAYS, STEPS), I32),
             jax.ShapeDtypeStruct((64, 128), F32),
         ),
-        in_specs=[SM, VM, VM, VM, VM],
-        out_specs=(VM, VM, VM),
+        in_specs=[VM, VM, VM, VM],
+        out_specs=(VM, VM, VM, VM),
         scratch_shapes=[
             pltpu.VMEM((257, 8, 128), F32),
             pltpu.VMEM((8192, 8), F32),
@@ -381,8 +385,8 @@
             pltpu.SMEM((WAYS, STEPS), I32),
             pltpu.SemaphoreType.DMA,
         ],
-        compiler_params=pltpu.CompilerParams(vmem_limit_bytes=48 << 20),
-    )(pair_count, pair_tiles, own, extra, ghost)
+        compiler_params=pltpu.CompilerParams(vmem_limit_bytes=24 << 20),
+    )(columns, own, extra, ghost)
 
 
 def force_step(codes, own, ghost, density, ghost_density, rank):
@@ -394,13 +398,16 @@
         out_specs=(VM, VM),
         scratch_shapes=[pltpu.VMEM((257, 16, 128), F32), pltpu.VMEM((8192, 16), F32)]
         + [pltpu.VMEM((8192, 128), F32)] * 4,
-        compiler_params=pltpu.CompilerParams(vmem_limit_bytes=48 << 20),
+        compiler_params=pltpu.CompilerParams(vmem_limit_bytes=40 << 20),
     )(codes, own, ghost, density, ghost_density, rank)
 
 
 LEVELS = 4
 SEND = 2048
 PIECE = 512
+BLOCK = 1024
+DENSE = 512
+DENSE_X = 512
 PIECES = SEND // PIECE
 GHOSTS = 1024
 MESH = pl.DeviceIdType.MESH
@@ -416,6 +423,13 @@
     i = (lax.axis_index("gx") + sign * (cell // 3 - 1) + count_x) % count_x
     j = (lax.axis_index("gy") + sign * (cell % 3 - 1) + count_y) % count_y
     return i, j
+
+
+def spread_state(own, parts):
+    for h in range(0, 32, 2):
+        pair = jnp.concatenate([own[:, h * 256 : h * 256 + 256], own[:, h * 256 + 256 : h * 256 + 512]], axis=0)
+        for n, part in enumerate(split3(pair)):
+            parts[n, h * 8 : h * 8 + 16, :] = part
 
 
 def permuted(value, lanes):
@@ -444,6 +458,13 @@
     index = jnp.broadcast_to(index, (8, 128))
     low = jnp.bitwise_and(index, 127)
     return chosen(lambda c: permuted(state[:, 128 * c : 128 * c + 128], low), digits_of(index >> 7, 6), 0, 64)
+
+
+def rows_by_matmul(parts, index):
+    hot = one_hot(index)
+    found = dot(parts[2], hot) + dot(parts[1], hot) + dot(parts[0], hot)
+    bits = digits_of(jnp.broadcast_to(index, (8, 256)) >> 8, 5)
+    return chosen(lambda h: found[8 * h : 8 * h + 8], bits, 0, 32)
 
 
 def pairs_at(extra, index, groups):
@@ -471,8 +492,9 @@
     return jnp.where(slot >= 0, new, old)
 
 
-def exchange_kernel(count_x, count_y, counts, particles, extra_in, rows, exports, own, extra, ghost,
-                    hot, inverse, inverse_wide, slots, slots_x, exports_3, base_main, base_extra,
+def exchange_kernel(count_x, count_y, counts, used, particles_h, old_h, active_h, rows_h, exports_h, pairs_h,
+                    own, extra, ghost, columns, exports_3,
+                    loads, old, active, rows, exports, pairs, parts, hot, inverse, inverse_wide, slots, slots_x, base_main, base_extra,
                     send_main, send_extra, recv_main, recv_extra, recv_wide,
                     send_ghost, send_sems, recv_sems, ghost_send, ghost_recv):
     i, j = lax.axis_index("gx"), lax.axis_index("gy")
@@ -483,6 +505,14 @@
         (i, flipped(j, bits_y - 1)),
         (i, flipped(j, bits_y - 2)),
     ]
+    copies = [
+        pltpu.make_async_copy(source, target, loads.at[n])
+        for n, (source, target) in enumerate(
+            ((rows_h, rows), (particles_h, own), (old_h, old), (active_h, active), (exports_h, exports), (pairs_h, pairs))
+        )
+    ]
+    for copy in copies:
+        copy.start()
     barrier = pltpu.get_barrier_semaphore()
     for partner in partners:
         pl.semaphore_signal(barrier, inc=1, device_id=partner, device_id_type=MESH)
@@ -492,7 +522,7 @@
     def invert(level):
         slot = iota((32, SEND), 1)
         index = rows[level : level + 1, :]
-        high = jnp.where(slot < counts[level, 0], jnp.broadcast_to(index >> 8, (32, SEND)), 64)
+        high = jnp.where(slot < counts[0, level], jnp.broadcast_to(index >> 8, (32, SEND)), 64)
         here = iota((32, SEND), 0) == high
         digits = jnp.concatenate(
             [
@@ -544,13 +574,18 @@
         )
 
     def gather(level, out):
-        @pl.loop(0, PIECES)
-        def _(piece):
-            for k in range(PIECE // 128):
-                at = pl.multiple_of(piece * PIECE + 128 * k, 128)
-                index = rows[level : level + 1, pl.ds(at, 128)]
-                out[:, pl.ds(at, 128)] = rows_at(own, index)
-                base_extra[:, pl.ds(at, 128)] = pairs_at(extra, index, 16)
+        spread_state(own, parts)
+
+        @pl.loop(0, SEND // BLOCK)
+        def _(block):
+            at = pl.multiple_of(block * BLOCK, BLOCK)
+            for k in range(0, DENSE, 256):
+                out[:, pl.ds(at + k, 256)] = rows_by_matmul(parts, rows[level : level + 1, pl.ds(at + k, 256)])
+            for k in range(0, BLOCK, 128):
+                index = rows[level : level + 1, pl.ds(at + k, 128)]
+                base_extra[:, pl.ds(at + k, 128)] = pairs_at(extra, index, 16)
+                if k >= DENSE:
+                    out[:, pl.ds(at + k, 128)] = rows_at(own, index)
 
     def compose(level):
         @pl.loop(0, PIECES)
@@ -586,20 +621,26 @@
             wide = jnp.concatenate([recv_extra[level, 2 * c : 2 * c + 2, :]] * 4, axis=0)
             recv_wide[:, 128 * c : 128 * c + 128] = wide
 
-        @pl.loop(0, 16)
-        def _(g):
-            at = pl.multiple_of(g * 8, 8)
-            slot = inverse_wide[level, pl.ds(at, 8), :]
-            extra[pl.ds(at, 8), :] = landed(lambda c: recv_wide[:, 128 * c : 128 * c + 128], slot, extra[pl.ds(at, 8), :])
-            for b in range(4):
-                lanes = pl.ds(pl.multiple_of(g * 512, 512) + 128 * b, 128)
-                slot_b = jnp.broadcast_to(slot[2 * b : 2 * b + 1], (8, 128))
-                own[:, lanes] = landed(
-                    lambda c: recv_main[level, :, 128 * c : 128 * c + 128], slot_b, own[:, lanes]
+        @pl.loop(0, 8)
+        def _(step):
+            for late in range(2):
+                g = step * 2 + late
+                at = pl.multiple_of(g * 8, 8)
+                slot = inverse_wide[level, pl.ds(at, 8), :]
+                extra[pl.ds(at, 8), :] = landed(
+                    lambda c: recv_wide[:, 128 * c : 128 * c + 128], slot, extra[pl.ds(at, 8), :]
                 )
-
-    own[...] = particles[...]
-    extra[...] = extra_in[...]
+                for b in range(4):
+                    lanes = pl.ds(pl.multiple_of(g * 512, 512) + 128 * b, 128)
+                    slot_b = jnp.broadcast_to(slot[2 * b : 2 * b + 1], (8, 128))
+                    own[:, lanes] = landed(
+                        lambda c: recv_main[level, :, 128 * c : 128 * c + 128], slot_b, own[:, lanes]
+                    )
+
+    for copy in copies:
+        copy.wait()
+    extra[pl.ds(0, 64, stride=2), :] = old[...]
+    extra[pl.ds(1, 64, stride=2), :] = active[...].astype(F32)
     for number in range(8):
         exports_3[number] = exports[number : number + 1, :]
     gather(0, send_main.at[0])
@@ -607,6 +648,8 @@
 
     for level in range(LEVELS):
         send(level)
+        if level == 0:
+            columns[...] = pair_columns(pairs[...].astype(F32), used[0])
         invert(level)
         if level > 0:
             settle(level - 1)
@@ -615,14 +658,18 @@
             gather(level + 1, base_main)
         else:
 
-            @pl.loop(0, 16)
-            def _(block):
-                number, part = block // 2, block % 2
-                for k in range(4):
-                    lanes = pl.multiple_of(part * 512 + 128 * k, 128)
-                    index = exports_3[number, :, pl.ds(lanes, 128)]
-                    slots_x[number, :, pl.ds(lanes, 128)] = cells_at(inverse, index)
-                    send_ghost[:, pl.ds(pl.multiple_of(number * GHOSTS + lanes, 128), 128)] = rows_at(own, index)
+            spread_state(own, parts)
+
+            @pl.loop(0, 8)
+            def _(number):
+                at = pl.multiple_of(number * GHOSTS, GHOSTS)
+                for k in range(0, DENSE_X, 256):
+                    send_ghost[:, pl.ds(at + k, 256)] = rows_by_matmul(parts, exports_3[number, :, k : k + 256])
+                for k in range(0, GHOSTS, 128):
+                    index = exports_3[number, :, k : k + 128]
+                    slots_x[number, :, k : k + 128] = cells_at(inverse, index)
+                    if k >= DENSE_X:
+                        send_ghost[:, pl.ds(at + k, 128)] = rows_at(own, index)
 
         arrive(level)
 
@@ -641,7 +688,10 @@
         ghost_copy(number).wait()
 
 
-def exchange(mesh, send_count, particles, extra, send_rows, export_rows):
+HB = pl.BlockSpec(memory_space=pltpu.HBM)
+
+
+def exchange(mesh, send_count, pair_count, particles, old, active, send_rows, export_rows, pair_tiles):
     count_x, count_y = mesh.shape["gx"], mesh.shape["gy"]
     return pl.pallas_call(
         functools.partial(exchange_kernel, count_x, count_y),
@@ -650,15 +700,23 @@
             jax.ShapeDtypeStruct((8, 8192), F32),
             jax.ShapeDtypeStruct((128, 128), F32),
             jax.ShapeDtypeStruct((8, 8192), F32),
+            jax.ShapeDtypeStruct((8, COLS), F32),
+            jax.ShapeDtypeStruct((8, 1, GHOSTS), I32),
         ),
-        in_specs=[SM, VM, VM, VM, VM],
-        out_specs=(VM, VM, VM),
+        in_specs=[SM, SM, HB, HB, HB, HB, HB, HB],
+        out_specs=(VM, VM, VM, VM, VM),
         scratch_shapes=[
+            pltpu.SemaphoreType.DMA((6,)),
+            pltpu.VMEM((64, 128), F32),
+            pltpu.VMEM((64, 128), I32),
+            pltpu.VMEM((LEVELS, SEND), I32),
+            pltpu.VMEM((8, GHOSTS), I32),
+            pltpu.VMEM((2, 512), I32),
+            pltpu.VMEM((3, 256, 256), BF16),
             pltpu.VMEM((256, SEND), BF16),
             pltpu.VMEM((64, 128), I32),
             pltpu.VMEM((LEVELS, 128, 128), I32),
             pltpu.VMEM((1, SEND), I32),
-            pltpu.VMEM((8, 1, GHOSTS), I32),
             pltpu.VMEM((8, 1, GHOSTS), I32),
             pltpu.VMEM((8, SEND), F32),
             pltpu.VMEM((8, SEND), F32),
@@ -674,17 +732,16 @@
             pltpu.SemaphoreType.DMA((8,)),
         ],
         compiler_params=pltpu.CompilerParams(
-            collective_id=0, has_side_effects=True, vmem_limit_bytes=48 << 20
+            collective_id=0, has_side_effects=True, vmem_limit_bytes=24 << 20
         ),
-    )(send_count, particles, extra, send_rows, export_rows)
-
-
-def ghost_density_kernel(count_x, count_y, density, exports, out, exports_3, send, send_sems, recv_sems):
+    )(send_count, pair_count, particles, old, active, send_rows, export_rows, pair_tiles)
+
+
+def ghost_density_kernel(count_x, count_y, density, exports_3, out, send, send_sems, recv_sems):
     barrier = pltpu.get_barrier_semaphore()
     for number in range(8):
         pl.semaphore_signal(barrier, inc=1, device_id=neighbour(number, 1, count_x, count_y), device_id_type=MESH)
-    for number in range(8):
-        exports_3[number] = exports[number : number + 1, :]
+
     def copy(number):
         return pltpu.make_async_remote_copy(
             src_ref=send.at[number],
@@ -720,24 +777,32 @@
         in_specs=[VM, VM],
         out_specs=VM,
         scratch_shapes=[
-            pltpu.VMEM((8, 1, GHOSTS), I32),
             pltpu.VMEM((8, 8, 128), F32),
             pltpu.SemaphoreType.DMA((8,)),
             pltpu.SemaphoreType.DMA((8,)),
         ],
-        compiler_params=pltpu.CompilerParams(collective_id=1, has_side_effects=True, vmem_limit_bytes=32 << 20),
+        compiler_params=pltpu.CompilerParams(collective_id=1, has_side_effects=True, vmem_limit_bytes=8 << 20),
     )(density, export_rows)
 
 
 def on_device(
     mesh, particles, old_density, active, send_rows, send_count, export_rows, pair_tiles, pair_count
 ):
-    extra = jnp.stack([old_density.reshape(64, 128), active.astype(F32).reshape(64, 128)], axis=1).reshape(128, 128)
-    own, extra, ghost = exchange(mesh, send_count, particles, extra, send_rows, export_rows)
-    density, codes, rank = density_step(pair_count, pair_tiles, own, extra, ghost)
-    ghost_density = ghost_density_step(mesh, density, export_rows).reshape(64, 128)
+    own, extra, ghost, columns, exports = exchange(
+        mesh,
+        send_count.T,
+        pair_count,
+        particles,
+        old_density.reshape(64, 128),
+        active.reshape(64, 128),
+        send_rows,
+        export_rows,
+        pair_tiles,
+    )
+    result, density, codes, rank = density_step(columns, own, extra, ghost)
+    ghost_density = ghost_density_step(mesh, density, exports).reshape(64, 128)
     acceleration, heating = force_step(codes, own, ghost, density, ghost_density, rank)
-    return density.reshape(8192), acceleration, heating.reshape(8192)
+    return result.reshape(8192), acceleration, heating.reshape(8192)
 
 
 def solution(mesh):

time: 107 us -> 101 us (0.944)
  Pallas kernels: 100 us -> 94.6 us
    pallas_call x1, Pallas kernels: 45.3 us -> 39.9 us  [exchange(): pl.pallas_call(functools.partial(exchange_kernel, count_x, count_y), name...]
    unnamed x17 -> x14, local copies, waits for them, and re-layouts: 3.83 us -> 4.63 us
where the time goes in v2:
time: 101 us
  Pallas kernels  94.6 us (94%)
  local copies, waits for them, and re-layouts  4.63 us (5%)
  between operations  1.34 us (1%)
    pallas_call x1, Pallas kernels, exchange(): pl.pallas_call(functools.partial(exchange_kernel, count_x, count_y), name...  39.9 us
    pallas_call x1, Pallas kernels, force_step(): pl.pallas_call(force_kernel, name='force', out_shape=(jax.ShapeDtypeStruc...  26.7 us
    pallas_call x1, Pallas kernels, density_step(): pl.pallas_call(density_kernel, name='density', out_shape=(jax.ShapeDtypeS...  17.8 us
    pallas_call x1, Pallas kernels, ghost_density_step(): pl.pallas_call(functools.partial(ghost_density_kernel, mesh.shape['gx'],...  10.1 us
    unnamed x14, local copies, waits for them, and re-layouts  4.63 us

profile of v2, /device:TPU:0, one launch (start us, length us, event | category | flops | bytes accessed | tf_op | source)
XLA Modules:
  0.0 100.5 jit_solution(939869746130048410)
XLA Ops:
  0.6 0.0 copy-start.5
  1.3 0.0 copy-start.6
  1.3 0.0 copy-done.5
  1.3 0.6 copy-done.6
  2.0 0.0 copy-start
  2.0 0.9 copy-done
  2.9 0.0 copy-start.1
  2.9 0.8 copy-done.1
  3.7 0.0 copy-start.2
  3.7 0.8 copy-done.2
  4.4 0.0 copy-start.3
  4.4 0.8 copy-done.3
  5.2 0.0 copy-start.4
  5.2 0.8 copy-done.4
  5.9 39.9 %exchange.1 = (f32[8,8192]{1,0:T(8,128)S(1)}, f32[128,128]{1,0:T(8,128)S(1)}, f32[8,8192]{1,0:T(8,128)S(1)}, f32[8,320]{1,0:T(8,128)S(1)}, s32[8,1,1024]{2,1,0:T(1,128)S(1)}) custom-call(s32[1,4]{1,0:T(1,128)S(1)} %bitcast.9, s32[1]{0:T(128)S(6)} %copy.11.used, f32[8,8192]{1,0:T(8,128)S(1)} %copy-done, f32[64,128]{1,0:T(8,128)S(1)} %bitcast.7, ...), custom_call_target="tpu_custom_call" | custom-call | tf_op jit(solution)/shard_map/exchange/pallas_call | solution.py:696
  45.9 17.8 %density.1 = (f32[64,128]{1,0:T(8,128)}, f32[64,128]{1,0:T(8,128)S(1)}, s32[8,384]{1,0:T(8,128)S(1)}, f32[64,128]{1,0:T(8,128)S(1)}) custom-call(f32[8,320]{1,0:T(8,128)S(1)} %get-tuple-element.14.cols_ref, f32[8,8192]{1,0:T(8,128)S(1)} %get-tuple-element.15.own_ref, f32[128,128]{1,0:T(8,128)S(1)} %get-tuple-element.16.extra_ref, ...), custom_call_target="tpu_custom_call" | custom-call | tf_op jit(solution)/shard_map/density/pallas_call | solution.py:368
  63.7 10.1 %ghost_density.1 = f32[8,8,128]{2,1,0:T(8,128)S(1)} custom-call(f32[64,128]{1,0:T(8,128)S(1)} %get-tuple-element.20.density.dens_ref, s32[8,1,1024]{2,1,0:T(1,128)S(1)} %get-tuple-element.21.exports_3), custom_call_target="tpu_custom_call" | custom-call | tf_op jit(solution)/shard_map/ghost_density/pallas_call | solution.py:773
  73.8 26.7 %force.1 = (f32[3,8192]{1,0:T(4,128)}, f32[64,128]{1,0:T(8,128)}) custom-call(s32[8,384]{1,0:T(8,128)S(1)} %get-tuple-element.19.code_ref, f32[8,8192]{1,0:T(8,128)S(1)} %get-tuple-element.15.own_ref, f32[8,8192]{1,0:T(8,128)S(1)} %get-tuple-element.17.ghost_ref, f32[64,128]{1,0:T(8,128)S(1)} %get-tuple-element.20.density.dens_ref, f32[64,128]{1,0:T(8,128)S(1)} %bitcast.6, ...), custom_call_target="tpu_custom_call" | custom-call | tf_op jit(solution)/shard_map/force/pallas_call | solution.py:393
Async XLA Ops:
  0.6 0.7 copy-start.5
  1.3 0.7 copy-start.6
  2.0 0.9 copy-start
  2.9 0.8 copy-start.1
  3.7 0.8 copy-start.2
  4.4 0.8 copy-start.3
  5.2 0.8 copy-start.4

commit v3 on v2

--- a/solution.py
+++ b/solution.py
@@ -18,6 +18,7 @@
 COLS = 320
 STEPS = 384
 WAYS = 8
+SPAN = 8
 FEW = 4
 
 
@@ -129,26 +130,24 @@
     table[slot + 1] = jnp.where(left, other, chunk)
 
 
-def put_targets(columns, tile, chunk, rank, first, last):
-    left = iota(chunk.shape, 1) < 64
-    a, b, c = [v.astype(F32) for v in split3(chunk)]
-    ar, br, cr = swap_halves(a), swap_halves(b), swap_halves(c)
-    zero = jnp.zeros_like(a)
+def put_targets(columns, chunk, fields, rank, first, last):
+    parts = jnp.concatenate([part.astype(F32) for part in split3(fields)], axis=0)
+    parts = jnp.concatenate([parts, jnp.zeros((128 - parts.shape[0], 128), F32)], axis=0).astype(BF16)
     wide = jnp.broadcast_to(rank, (8, 128))
-    wide_other = swap_halves(wide)
-    left8 = iota((8, 128), 1) < 64
-    for half in range(2):
-        if half == 0:
-            right = jnp.concatenate([jnp.where(left, a, br), jnp.where(left, c, zero)], axis=1)
-            own = jnp.where(left8, wide, wide_other)
-        else:
-            right = jnp.concatenate([jnp.where(left, ar, b), jnp.where(left, cr, zero)], axis=1)
-            own = jnp.where(left8, wide_other, wide)
-        sub = iota((8, 128), 0).astype(F32)
-        pick = jnp.concatenate([jnp.where(own == sub + 8.0 * g, 1.0, 0.0) for g in range(first, last)], axis=0).astype(BF16)
-        rows = dot_nt(jnp.concatenate([pick, pick], axis=1), right.astype(BF16))
-        for g in range(first, last):
-            columns[pl.ds(g * 1024 + (tile + half) * 8, 8), :] = rows[8 * (g - first) : 8 * (g - first) + 8]
+    left = iota((8, 128), 1) < 64
+    sub = iota((8, 128), 0).astype(F32)
+    ours = jnp.where(left, wide, -1.0), jnp.where(left, -1.0, wide)
+    pick = jnp.concatenate(
+        [jnp.where(our == sub + 8.0 * g, 1.0, 0.0) for g in range(first, last) for our in ours], axis=0
+    ).astype(BF16)
+    rows = dot_nt(pick, parts)
+    for g in range(first, last):
+        columns[pl.ds(g * 1024 + chunk * 16, 16), :] = rows[16 * (g - first) : 16 * (g - first) + 16]
+
+
+def widener(fields, stride):
+    k, n = iota((128, 128 * fields), 0), iota((128, 128 * fields), 1)
+    return ((k % stride == n // 128) & (k < 3 * stride)).astype(F32).astype(BF16)
 
 
 def gather_sums(totals, tile, rank, first, last):
@@ -174,32 +173,21 @@
     return code & 1023, (code >> 10) & 511, code >> 19
 
 
-def density_item(code, columns, sources):
-    place, one, two = decode(code)
-    row = pl.multiple_of(place * 8, 8)
-    mine = columns[pl.ds(row, 8), :]
-    left = iota((8, 128), 1) < 64
-    other = jnp.where(left, sources[one], sources[two])
-    dx = wrapped(mine[:, 0:1], other[0:1])
-    dy = wrapped(mine[:, 1:2], other[1:2])
-    dz = wrapped(mine[:, 2:3], other[2:3])
+def density_item(mine, other):
+    dx = wrapped(mine[0], other[0:1])
+    dy = wrapped(mine[1], other[1:2])
+    dz = wrapped(mine[2], other[2:3])
     rsq = jnp.maximum(dx * dx + dy * dy + dz * dz, other[3:4])
-    q = rsq * lax.rsqrt(rsq) * mine[:, 3:4]
+    q = rsq * lax.rsqrt(rsq) * mine[3]
     t = jnp.maximum(2.0 - q, 0.0)
     u = jnp.maximum(1.0 - q, 0.0)
-    w = t * t * t - 4.0 * (u * u * u)
-    return row, w
-
-
-def force_item(code, columns, sources):
-    place, one, two = decode(code)
-    row = pl.multiple_of(place * 8, 8)
-    mine = columns[pl.ds(row, 8), :]
-    left = iota((16, 128), 1) < 64
-    other = jnp.where(left, sources[one], sources[two])
-    dx = wrapped(mine[:, 0:1], other[0:1])
-    dy = wrapped(mine[:, 1:2], other[1:2])
-    dz = wrapped(mine[:, 2:3], other[2:3])
+    return (t * t * t - 4.0 * (u * u * u),)
+
+
+def force_item(mine, other):
+    dx = wrapped(mine[0], other[0:1])
+    dy = wrapped(mine[1], other[1:2])
+    dz = wrapped(mine[2], other[2:3])
     rsq = jnp.maximum(dx * dx + dy * dy + dz * dz, other[10:11])
     inv = lax.rsqrt(rsq)
     r = rsq * inv
@@ -209,14 +197,10 @@
         t = jnp.maximum(2.0 - q, 0.0)
         return jnp.where(q < 1.0, 4.0 - 3.0 * q, t * t * (h * inv))
 
-    slope = profile(mine[:, 6:7], mine[:, 8:9]) * mine[:, 9:10] + profile(other[6:7], other[8:9]) * other[9:10]
-    w = (mine[:, 7:8] + other[7:8]) * slope
-    gap = (
-        (mine[:, 3:4] - other[3:4]) * dx
-        + (mine[:, 4:5] - other[4:5]) * dy
-        + (mine[:, 5:6] - other[5:6]) * dz
-    )
-    return row, (w * dx, w * dy, w * dz, w * gap)
+    slope = profile(mine[6], mine[8]) * mine[9] + profile(other[6:7], other[8:9]) * other[9:10]
+    w = (mine[7] + other[7:8]) * slope
+    gap = (mine[3] - other[3:4]) * dx + (mine[4] - other[4:5]) * dy + (mine[5] - other[5:6]) * dz
+    return (w * dx, w * dy, w * dz, w * gap)
 
 
 def for_all_groups(most, body):
@@ -227,17 +211,26 @@
         body(FEW, 8, True)
 
 
-def run_items(number, codes, item):
-    @pl.loop(0, (number + 2 * WAYS - 1) // (2 * WAYS))
-    def _(pair):
-        for late in range(2):
-            for way in range(WAYS):
-                item(codes[way, 2 * pair + late])
+def run_items(number, codes, columns, sources, spread, fields, item, totals):
+    @pl.loop(0, (number + SPAN * WAYS - 1) // (SPAN * WAYS))
+    def _(span):
+        for late in range(0, SPAN, 2):
+            places = [decode(codes[way, SPAN * span + late + n]) for n in range(2) for way in range(WAYS)]
+            rows = [pl.multiple_of(place * 8, 8) for place, _, _ in places]
+            mine = jnp.concatenate([columns[pl.ds(row, 8), :] for row in rows], axis=0).astype(BF16)
+            wide = dot(mine, spread[...])
+            for n, (_, one, two) in enumerate(places):
+                first, second = sources[one], sources[two]
+                other = jnp.where(iota(first.shape, 1) < 64, first, second)
+                own = [wide[8 * n : 8 * n + 8, 128 * f : 128 * f + 128] for f in range(fields)]
+                for total, term in zip(totals, item(own, other)):
+                    total[pl.ds(rows[n], 8), :] += term
 
 
 def density_kernel(cols_ref, own_ref, extra_ref, ghost_ref, result_ref, dens_ref, code_ref, rank_ref,
-                   sources, columns, total, sums, smooth, codes_s, sem):
+                   sources, columns, spread, total, sums, smooth, codes_s, sem):
     active = extra_ref[pl.ds(1, 64, stride=2), :]
+    spread[...] = widener(4, 8)
     rank_ref[...] = ranks_of(active)
     code_ref[...] = item_codes(cols_ref[...], tile_groups(active))
     copy = pltpu.make_async_copy(code_ref, codes_s, sem)
@@ -271,17 +264,13 @@
             for part in range(4):
                 chunk = step * 4 + part
                 lanes = pl.ds(pl.multiple_of(step * 512, 512) + 128 * part, 128)
-                put_targets(columns, chunk * 2, targets(own_ref[:, lanes]), rank_ref[pl.ds(chunk, 1), :], first, last)
+                put_targets(columns, chunk, targets(own_ref[:, lanes]), rank_ref[pl.ds(chunk, 1), :], first, last)
                 for g in range(first, last):
                     total[pl.ds(g * 1024 + chunk * 16, 16), :] = jnp.zeros((16, 128), F32)
 
     for_all_groups(most, prepare)
 
-    def item(code):
-        row, w = density_item(code, columns, sources)
-        total[pl.ds(row, 8), :] += w
-
-    run_items(number, codes_s, item)
+    run_items(number, codes_s, columns, sources, spread, 4, density_item, (total,))
 
     def collect(first, last, again):
         @pl.loop(0, 16)
@@ -301,8 +290,9 @@
 
 
 def force_kernel(code_ref, own_ref, ghost_ref, dens_ref, gdens_ref, rank_ref, acc_ref, heat_ref,
-                 sources, columns, ax, ay, az, heat):
+                 sources, columns, spread, ax, ay, az, heat):
     number, most = code_ref[0, STEPS - 1], code_ref[0, STEPS - 2]
+    spread[...] = widener(10, 16)
 
     def fields(block, density):
         h = block[6:7]
@@ -329,7 +319,7 @@
         def _(step):
             for part in range(4):
                 chunk = step * 4 + part
-                put_targets(columns, chunk * 2, own_fields(step, part), rank_ref[pl.ds(chunk, 1), :], first, last)
+                put_targets(columns, chunk, own_fields(step, part), rank_ref[pl.ds(chunk, 1), :], first, last)
                 for g in range(first, last):
                     for total in (ax, ay, az, heat):
                         total[pl.ds(g * 1024 + chunk * 16, 16), :] = jnp.zeros((16, 128), F32)
@@ -338,12 +328,7 @@
     sub = iota((16, 128), 0)
     sources[256] = jnp.where(sub == 10, FAR, jnp.where((sub == 6) | (sub == 8), 1.0, 0.0))
 
-    def item(code):
-        row, terms = force_item(code, columns, sources)
-        for total, term in zip((ax, ay, az, heat), terms):
-            total[pl.ds(row, 8), :] += term
-
-    run_items(number, code_ref, item)
+    run_items(number, code_ref, columns, sources, spread, 10, force_item, (ax, ay, az, heat))
 
     def collect(first, last, again):
         @pl.loop(0, 16)
@@ -378,7 +363,8 @@
         out_specs=(VM, VM, VM, VM),
         scratch_shapes=[
             pltpu.VMEM((257, 8, 128), F32),
-            pltpu.VMEM((8192, 8), F32),
+            pltpu.VMEM((8192, 128), F32),
+            pltpu.VMEM((128, 512), BF16),
             pltpu.VMEM((8192, 128), F32),
             pltpu.VMEM((64, 128), F32),
             pltpu.VMEM((64, 128), F32),
@@ -396,7 +382,7 @@
         out_shape=(jax.ShapeDtypeStruct((3, 8192), F32), jax.ShapeDtypeStruct((64, 128), F32)),
         in_specs=[SM, VM, VM, VM, VM, VM],
         out_specs=(VM, VM),
-        scratch_shapes=[pltpu.VMEM((257, 16, 128), F32), pltpu.VMEM((8192, 16), F32)]
+        scratch_shapes=[pltpu.VMEM((257, 16, 128), F32), pltpu.VMEM((8192, 128), F32), pltpu.VMEM((128, 1280), BF16)]
         + [pltpu.VMEM((8192, 128), F32)] * 4,
         compiler_params=pltpu.CompilerParams(vmem_limit_bytes=40 << 20),
     )(codes, own, ghost, density, ghost_density, rank)
@@ -492,9 +478,9 @@
     return jnp.where(slot >= 0, new, old)
 
 
-def exchange_kernel(count_x, count_y, counts, used, particles_h, old_h, active_h, rows_h, exports_h, pairs_h,
+def exchange_kernel(count_x, count_y, used, counts_h, particles_h, old_h, active_h, rows_h, exports_h, pairs_h,
                     own, extra, ghost, columns, exports_3,
-                    loads, old, active, rows, exports, pairs, parts, hot, inverse, inverse_wide, slots, slots_x, base_main, base_extra,
+                    loads, counts, old, active, rows, exports, pairs, parts, hot, inverse, inverse_wide, slots, slots_x, base_main, base_extra,
                     send_main, send_extra, recv_main, recv_extra, recv_wide,
                     send_ghost, send_sems, recv_sems, ghost_send, ghost_recv):
     i, j = lax.axis_index("gx"), lax.axis_index("gy")
@@ -508,7 +494,7 @@
     copies = [
         pltpu.make_async_copy(source, target, loads.at[n])
         for n, (source, target) in enumerate(
-            ((rows_h, rows), (particles_h, own), (old_h, old), (active_h, active), (exports_h, exports), (pairs_h, pairs))
+            ((rows_h, rows), (counts_h, counts), (particles_h, own), (old_h, old), (active_h, active), (exports_h, exports), (pairs_h, pairs))
         )
     ]
     for copy in copies:
@@ -522,7 +508,7 @@
     def invert(level):
         slot = iota((32, SEND), 1)
         index = rows[level : level + 1, :]
-        high = jnp.where(slot < counts[0, level], jnp.broadcast_to(index >> 8, (32, SEND)), 64)
+        high = jnp.where(slot < counts[0:1, level : level + 1], jnp.broadcast_to(index >> 8, (32, SEND)), 64)
         here = iota((32, SEND), 0) == high
         digits = jnp.concatenate(
             [
@@ -703,10 +689,11 @@
             jax.ShapeDtypeStruct((8, COLS), F32),
             jax.ShapeDtypeStruct((8, 1, GHOSTS), I32),
         ),
-        in_specs=[SM, SM, HB, HB, HB, HB, HB, HB],
+        in_specs=[SM, HB, HB, HB, HB, HB, HB, HB],
         out_specs=(VM, VM, VM, VM, VM),
         scratch_shapes=[
-            pltpu.SemaphoreType.DMA((6,)),
+            pltpu.SemaphoreType.DMA((7,)),
+            pltpu.VMEM((1, 4), I32),
             pltpu.VMEM((64, 128), F32),
             pltpu.VMEM((64, 128), I32),
             pltpu.VMEM((LEVELS, SEND), I32),
@@ -734,7 +721,13 @@
         compiler_params=pltpu.CompilerParams(
             collective_id=0, has_side_effects=True, vmem_limit_bytes=24 << 20
         ),
-    )(send_count, pair_count, particles, old, active, send_rows, export_rows, pair_tiles)
+    )(
+        pair_count,
+        *[
+            pltpu.with_memory_space_constraint(x, pltpu.HBM)
+            for x in (send_count, particles, old, active, send_rows, export_rows, pair_tiles)
+        ],
+    )
 
 
 def ghost_density_kernel(count_x, count_y, density, exports_3, out, send, send_sems, recv_sems):

time: 101 us -> 82.9 us (0.82)
  Pallas kernels: 94.6 us -> 81.1 us
  local copies, waits for them, and re-layouts: 4.63 us -> 0 us
    pallas_call x1, Pallas kernels: 26.7 us -> 19.6 us  [force_step(): pl.pallas_call(force_kernel, name='force', out_shape=(jax.ShapeDtypeStruc...]
    pallas_call x1, Pallas kernels: 17.8 us -> 12.9 us  [density_step(): pl.pallas_call(density_kernel, name='density', out_shape=(jax.ShapeDtypeS...]
    unnamed x14 -> x0, local copies, waits for them, and re-layouts: 4.63 us -> none
    pallas_call x1, Pallas kernels: 39.9 us -> 38.5 us  [exchange(): pl.pallas_call(functools.partial(exchange_kernel, count_x, count_y), name...]
where the time goes in v3:
time: 82.9 us; the launch traced here: 82.4 us
  Pallas kernels  81.1 us (98%)
  between operations  1.3 us (2%)
    pallas_call x1, Pallas kernels, exchange(): pl.pallas_call(functools.partial(exchange_kernel, count_x, count_y), name...  38.5 us
    pallas_call x1, Pallas kernels, force_step(): pl.pallas_call(force_kernel, name='force', out_shape=(jax.ShapeDtypeStruc...  19.6 us
    pallas_call x1, Pallas kernels, density_step(): pl.pallas_call(density_kernel, name='density', out_shape=(jax.ShapeDtypeS...  12.9 us
    pallas_call x1, Pallas kernels, ghost_density_step(): pl.pallas_call(functools.partial(ghost_density_kernel, mesh.shape['gx'],...  10.1 us

profile of v3, /device:TPU:0, one launch (start us, length us, event | category | flops | bytes accessed | tf_op | source)
XLA Modules:
  0.0 82.4 jit_solution(8695671917611915267)
XLA Ops:
  1.3 38.5 %exchange.1 = (f32[8,8192]{1,0:T(8,128)S(1)}, f32[128,128]{1,0:T(8,128)S(1)}, f32[8,8192]{1,0:T(8,128)S(1)}, f32[8,320]{1,0:T(8,128)S(1)}, s32[8,1,1024]{2,1,0:T(1,128)S(1)}) custom-call(s32[1]{0:T(128)S(6)} %copy.11.used, s32[1,4]{1,0:T(1,128)} %bitcast.9, f32[8,8192]{1,0:T(8,128)} %particles_h.1, f32[64,128]{1,0:T(8,128)} %bitcast.7, s32[64,128]{1,0:T(8,128)} %bitcast.8, ...), custom_call_target="tpu_custom_call" | custom-call | tf_op jit(solution)/shard_map/exchange/pallas_call | solution.py:682
  39.8 12.9 %density.1 = (f32[64,128]{1,0:T(8,128)}, f32[64,128]{1,0:T(8,128)S(1)}, s32[8,384]{1,0:T(8,128)S(1)}, f32[64,128]{1,0:T(8,128)S(1)}) custom-call(f32[8,320]{1,0:T(8,128)S(1)} %get-tuple-element.14.cols_ref, f32[8,8192]{1,0:T(8,128)S(1)} %get-tuple-element.15.own_ref, f32[128,128]{1,0:T(8,128)S(1)} %get-tuple-element.16.extra_ref, ...), custom_call_target="tpu_custom_call" | custom-call | tf_op jit(solution)/shard_map/density/pallas_call | solution.py:353
  52.7 10.1 %ghost_density.1 = f32[8,8,128]{2,1,0:T(8,128)S(1)} custom-call(f32[64,128]{1,0:T(8,128)S(1)} %get-tuple-element.20.density.dens_ref, s32[8,1,1024]{2,1,0:T(1,128)S(1)} %get-tuple-element.21.exports_3), custom_call_target="tpu_custom_call" | custom-call | tf_op jit(solution)/shard_map/ghost_density/pallas_call | solution.py:766
  62.9 19.6 %force.1 = (f32[3,8192]{1,0:T(4,128)}, f32[64,128]{1,0:T(8,128)}) custom-call(s32[8,384]{1,0:T(8,128)S(1)} %get-tuple-element.19.code_ref, f32[8,8192]{1,0:T(8,128)S(1)} %get-tuple-element.15.own_ref, f32[8,8192]{1,0:T(8,128)S(1)} %get-tuple-element.17.ghost_ref, f32[64,128]{1,0:T(8,128)S(1)} %get-tuple-element.20.density.dens_ref, f32[64,128]{1,0:T(8,128)S(1)} %bitcast.6, ...), custom_call_target="tpu_custom_call" | custom-call | tf_op jit(solution)/shard_map/force/pallas_call | solution.py:379

commit v4 on v3

--- a/solution.py
+++ b/solution.py
@@ -18,7 +18,8 @@
 COLS = 320
 STEPS = 384
 WAYS = 8
-SPAN = 8
+SPAN = 16
+TAIL = 4
 FEW = 4
 
 
@@ -212,19 +213,30 @@
 
 
 def run_items(number, codes, columns, sources, spread, fields, item, totals):
-    @pl.loop(0, (number + SPAN * WAYS - 1) // (SPAN * WAYS))
-    def _(span):
-        for late in range(0, SPAN, 2):
-            places = [decode(codes[way, SPAN * span + late + n]) for n in range(2) for way in range(WAYS)]
+    def steps(first, count):
+        for late in range(0, count, 2):
+            places = [decode(codes[way, first + late + n]) for n in range(2) for way in range(WAYS)]
             rows = [pl.multiple_of(place * 8, 8) for place, _, _ in places]
             mine = jnp.concatenate([columns[pl.ds(row, 8), :] for row in rows], axis=0).astype(BF16)
             wide = dot(mine, spread[...])
             for n, (_, one, two) in enumerate(places):
-                first, second = sources[one], sources[two]
-                other = jnp.where(iota(first.shape, 1) < 64, first, second)
+                first_tile, second_tile = sources[one], sources[two]
+                other = jnp.where(iota(first_tile.shape, 1) < 64, first_tile, second_tile)
                 own = [wide[8 * n : 8 * n + 8, 128 * f : 128 * f + 128] for f in range(fields)]
                 for total, term in zip(totals, item(own, other)):
                     total[pl.ds(rows[n], 8), :] += term
+
+    spans = number // (SPAN * WAYS)
+
+    @pl.loop(0, spans)
+    def _(span):
+        steps(SPAN * span, SPAN)
+
+    rest = number - spans * (SPAN * WAYS)
+
+    @pl.loop(0, (rest + TAIL * WAYS - 1) // (TAIL * WAYS))
+    def _(tail):
+        steps(SPAN * spans + TAIL * tail, TAIL)
 
 
 def density_kernel(cols_ref, own_ref, extra_ref, ghost_ref, result_ref, dens_ref, code_ref, rank_ref,
@@ -412,7 +424,7 @@
 
 
 def spread_state(own, parts):
-    for h in range(0, 32, 2):
+    for h in range(0, own.shape[1] // 256, 2):
         pair = jnp.concatenate([own[:, h * 256 : h * 256 + 256], own[:, h * 256 + 256 : h * 256 + 512]], axis=0)
         for n, part in enumerate(split3(pair)):
             parts[n, h * 8 : h * 8 + 16, :] = part
@@ -447,10 +459,11 @@
 
 
 def rows_by_matmul(parts, index):
+    blocks = parts.shape[1] // 8
     hot = one_hot(index)
     found = dot(parts[2], hot) + dot(parts[1], hot) + dot(parts[0], hot)
-    bits = digits_of(jnp.broadcast_to(index, (8, 256)) >> 8, 5)
-    return chosen(lambda h: found[8 * h : 8 * h + 8], bits, 0, 32)
+    bits = digits_of(jnp.broadcast_to(index, (8, 256)) >> 8, blocks.bit_length() - 1)
+    return chosen(lambda h: found[8 * h : 8 * h + 8], bits, 0, blocks)
 
 
 def pairs_at(extra, index, groups):
@@ -480,7 +493,7 @@
 
 def exchange_kernel(count_x, count_y, used, counts_h, particles_h, old_h, active_h, rows_h, exports_h, pairs_h,
                     own, extra, ghost, columns, exports_3,
-                    loads, counts, old, active, rows, exports, pairs, parts, hot, inverse, inverse_wide, slots, slots_x, base_main, base_extra,
+                    loads, counts, old, active, rows, exports, pairs, parts, parts_in, hot, inverse, inverse_wide, slots, slots_x, base_main, base_extra,
                     send_main, send_extra, recv_main, recv_extra, recv_wide,
                     send_ghost, send_sems, recv_sems, ghost_send, ghost_recv):
     i, j = lax.axis_index("gx"), lax.axis_index("gy")
@@ -603,25 +616,31 @@
             main_copy(level, piece).wait()
 
     def settle(level):
+        spread_state(recv_main.at[level], parts_in)
         for c in range(16):
             wide = jnp.concatenate([recv_extra[level, 2 * c : 2 * c + 2, :]] * 4, axis=0)
             recv_wide[:, 128 * c : 128 * c + 128] = wide
 
-        @pl.loop(0, 8)
+        @pl.loop(0, 4)
         def _(step):
-            for late in range(2):
-                g = step * 2 + late
+            for late in range(4):
+                g = step * 4 + late
                 at = pl.multiple_of(g * 8, 8)
                 slot = inverse_wide[level, pl.ds(at, 8), :]
                 extra[pl.ds(at, 8), :] = landed(
                     lambda c: recv_wide[:, 128 * c : 128 * c + 128], slot, extra[pl.ds(at, 8), :]
                 )
-                for b in range(4):
-                    lanes = pl.ds(pl.multiple_of(g * 512, 512) + 128 * b, 128)
+                first = pl.multiple_of(g * 512, 512)
+                for b in range(0, 2):
+                    lanes = pl.ds(first + 128 * b, 128)
                     slot_b = jnp.broadcast_to(slot[2 * b : 2 * b + 1], (8, 128))
                     own[:, lanes] = landed(
                         lambda c: recv_main[level, :, 128 * c : 128 * c + 128], slot_b, own[:, lanes]
                     )
+                lanes = pl.ds(first + 256, 256)
+                slot_row = jnp.concatenate([slot[4:5], slot[6:7]], axis=1)
+                fresh = rows_by_matmul(parts_in, slot_row)
+                own[:, lanes] = jnp.where(jnp.broadcast_to(slot_row, (8, 256)) >= 0, fresh, own[:, lanes])
 
     for copy in copies:
         copy.wait()
@@ -700,6 +719,7 @@
             pltpu.VMEM((8, GHOSTS), I32),
             pltpu.VMEM((2, 512), I32),
             pltpu.VMEM((3, 256, 256), BF16),
+            pltpu.VMEM((3, SEND // 32, 256), BF16),
             pltpu.VMEM((256, SEND), BF16),
             pltpu.VMEM((64, 128), I32),
             pltpu.VMEM((LEVELS, 128, 128), I32),
@@ -749,13 +769,13 @@
         for k in range(8):
             send[number, k : k + 1, :] = cells_at(density, exports_3[number, :, 128 * k : 128 * k + 128])
 
-    gathered(0)
+    @pl.loop(0, 2)
+    def _(half):
+        for n in range(4):
+            gathered(half * 4 + n)
+
     pl.semaphore_wait(barrier, 8)
-    copy(0).start()
-
-    @pl.loop(1, 8)
-    def _(number):
-        gathered(number)
+    for number in range(8):
         copy(number).start()
 
     for number in range(8):

time: 82.9 us -> 80.4 us (0.970)
  Pallas kernels: 81.1 us -> 79 us
    pallas_call x1, Pallas kernels: 38.5 us -> 37.1 us  [exchange(): pl.pallas_call(functools.partial(exchange_kernel, count_x, count_y), name...]
    pallas_call x1, Pallas kernels: 10.1 us -> 8.85 us  [ghost_density_step(): pl.pallas_call(functools.partial(ghost_density_kernel, mesh.shape['gx'],...]
where the time goes in v4:
time: 80.4 us; the launch traced here: 80.3 us
  Pallas kernels  79 us (98%)
  between operations  1.3 us (2%)
    pallas_call x1, Pallas kernels, exchange(): pl.pallas_call(functools.partial(exchange_kernel, count_x, count_y), name...  37.1 us
    pallas_call x1, Pallas kernels, force_step(): pl.pallas_call(force_kernel, name='force', out_shape=(jax.ShapeDtypeStruc...  20.2 us
    pallas_call x1, Pallas kernels, density_step(): pl.pallas_call(density_kernel, name='density', out_shape=(jax.ShapeDtypeS...  12.8 us
    pallas_call x1, Pallas kernels, ghost_density_step(): pl.pallas_call(functools.partial(ghost_density_kernel, mesh.shape['gx'],...  8.85 us

profile of v4, /device:TPU:0, one launch (start us, length us, event | category | flops | bytes accessed | tf_op | source)
XLA Modules:
  0.0 80.3 jit_solution(17709934799620539516)
XLA Ops:
  1.3 37.1 %exchange.1 = (f32[8,8192]{1,0:T(8,128)S(1)}, f32[128,128]{1,0:T(8,128)S(1)}, f32[8,8192]{1,0:T(8,128)S(1)}, f32[8,320]{1,0:T(8,128)S(1)}, s32[8,1,1024]{2,1,0:T(1,128)S(1)}) custom-call(s32[1]{0:T(128)S(6)} %copy.11.used, s32[1,4]{1,0:T(1,128)} %bitcast.9, f32[8,8192]{1,0:T(8,128)} %particles_h.1, f32[64,128]{1,0:T(8,128)} %bitcast.7, s32[64,128]{1,0:T(8,128)} %bitcast.8, ...), custom_call_target="tpu_custom_call" | custom-call | tf_op jit(solution)/shard_map/exchange/pallas_call | solution.py:701
  38.4 12.8 %density.1 = (f32[64,128]{1,0:T(8,128)}, f32[64,128]{1,0:T(8,128)S(1)}, s32[8,384]{1,0:T(8,128)S(1)}, f32[64,128]{1,0:T(8,128)S(1)}) custom-call(f32[8,320]{1,0:T(8,128)S(1)} %get-tuple-element.14.cols_ref, f32[8,8192]{1,0:T(8,128)S(1)} %get-tuple-element.15.own_ref, f32[128,128]{1,0:T(8,128)S(1)} %get-tuple-element.16.extra_ref, ...), custom_call_target="tpu_custom_call" | custom-call | tf_op jit(solution)/shard_map/density/pallas_call | solution.py:365
  51.3 8.8 %ghost_density.1 = f32[8,8,128]{2,1,0:T(8,128)S(1)} custom-call(f32[64,128]{1,0:T(8,128)S(1)} %get-tuple-element.20.density.dens_ref, s32[8,1,1024]{2,1,0:T(1,128)S(1)} %get-tuple-element.21.exports_3), custom_call_target="tpu_custom_call" | custom-call | tf_op jit(solution)/shard_map/ghost_density/pallas_call | solution.py:786
  60.1 20.2 %force.1 = (f32[3,8192]{1,0:T(4,128)}, f32[64,128]{1,0:T(8,128)}) custom-call(s32[8,384]{1,0:T(8,128)S(1)} %get-tuple-element.19.code_ref, f32[8,8192]{1,0:T(8,128)S(1)} %get-tuple-element.15.own_ref, f32[8,8192]{1,0:T(8,128)S(1)} %get-tuple-element.17.ghost_ref, f32[64,128]{1,0:T(8,128)S(1)} %get-tuple-element.20.density.dens_ref, f32[64,128]{1,0:T(8,128)S(1)} %bitcast.6, ...), custom_call_target="tpu_custom_call" | custom-call | tf_op jit(solution)/shard_map/force/pallas_call | solution.py:391

commit v5 on v4

--- a/solution.py
+++ b/solution.py
@@ -131,7 +131,11 @@
     table[slot + 1] = jnp.where(left, other, chunk)
 
 
-def put_targets(columns, chunk, fields, rank, first, last):
+def start_of(group):
+    return 8.0 * group if isinstance(group, int) else (8 * group).astype(F32)
+
+
+def put_targets(columns, chunk, fields, rank, groups):
     parts = jnp.concatenate([part.astype(F32) for part in split3(fields)], axis=0)
     parts = jnp.concatenate([parts, jnp.zeros((128 - parts.shape[0], 128), F32)], axis=0).astype(BF16)
     wide = jnp.broadcast_to(rank, (8, 128))
@@ -139,11 +143,11 @@
     sub = iota((8, 128), 0).astype(F32)
     ours = jnp.where(left, wide, -1.0), jnp.where(left, -1.0, wide)
     pick = jnp.concatenate(
-        [jnp.where(our == sub + 8.0 * g, 1.0, 0.0) for g in range(first, last) for our in ours], axis=0
+        [jnp.where(our == sub + start_of(g), 1.0, 0.0) for g in groups for our in ours], axis=0
     ).astype(BF16)
     rows = dot_nt(pick, parts)
-    for g in range(first, last):
-        columns[pl.ds(g * 1024 + chunk * 16, 16), :] = rows[16 * (g - first) : 16 * (g - first) + 16]
+    for n, g in enumerate(groups):
+        columns[pl.ds(pl.multiple_of(g * 1024 + chunk * 16, 16), 16), :] = rows[16 * n : 16 * n + 16]
 
 
 def widener(fields, stride):
@@ -151,16 +155,16 @@
     return ((k % stride == n // 128) & (k < 3 * stride)).astype(F32).astype(BF16)
 
 
-def gather_sums(totals, tile, rank, first, last):
+def gather_sums(totals, tile, rank, groups):
     left = iota((8, 128), 1) < 64
     wide = jnp.broadcast_to(rank, (8, 128))
     sub = iota((8, 128), 0).astype(F32)
     out = [jnp.zeros((8, 128), F32) for _ in totals]
-    for g in range(first, last):
-        hit = wide == sub + 8.0 * g
+    for g in groups:
+        hit = wide == sub + start_of(g)
         for n, total in enumerate(totals):
-            one = jnp.sum(total[pl.ds(g * 1024 + tile * 8, 8), :], axis=1, keepdims=True)
-            two = jnp.sum(total[pl.ds(g * 1024 + tile * 8 + 8, 8), :], axis=1, keepdims=True)
+            one = jnp.sum(total[pl.ds(pl.multiple_of(g * 1024 + tile * 8, 8), 8), :], axis=1, keepdims=True)
+            two = jnp.sum(total[pl.ds(pl.multiple_of(g * 1024 + tile * 8 + 8, 8), 8), :], axis=1, keepdims=True)
             out[n] = out[n] + jnp.where(hit, jnp.where(left, one, two), 0.0)
     return [jnp.sum(o, axis=0, keepdims=True) for o in out]
 
@@ -205,11 +209,11 @@
 
 
 def for_all_groups(most, body):
-    body(0, FEW, False)
-
-    @pl.when(most > FEW)
-    def _():
-        body(FEW, 8, True)
+    body(range(FEW), False)
+
+    @pl.loop(FEW, jnp.maximum(most, FEW))
+    def _(g):
+        body([g], True)
 
 
 def run_items(number, codes, columns, sources, spread, fields, item, totals):
@@ -270,26 +274,30 @@
     copy.wait()
     number, most = codes_s[0, STEPS - 1], codes_s[0, STEPS - 2]
 
-    def prepare(first, last, again):
-        @pl.loop(0, 16)
+    def prepare(groups, again):
+        per = 16 if again else 4
+
+        @pl.loop(0, 64 // per)
         def _(step):
-            for part in range(4):
-                chunk = step * 4 + part
-                lanes = pl.ds(pl.multiple_of(step * 512, 512) + 128 * part, 128)
-                put_targets(columns, chunk, targets(own_ref[:, lanes]), rank_ref[pl.ds(chunk, 1), :], first, last)
-                for g in range(first, last):
-                    total[pl.ds(g * 1024 + chunk * 16, 16), :] = jnp.zeros((16, 128), F32)
+            for part in range(per):
+                chunk = step * per + part
+                lanes = pl.ds(pl.multiple_of(step * (128 * per), 128 * per) + 128 * part, 128)
+                put_targets(columns, chunk, targets(own_ref[:, lanes]), rank_ref[pl.ds(chunk, 1), :], groups)
+                for g in groups:
+                    total[pl.ds(pl.multiple_of(g * 1024 + chunk * 16, 16), 16), :] = jnp.zeros((16, 128), F32)
 
     for_all_groups(most, prepare)
 
     run_items(number, codes_s, columns, sources, spread, 4, density_item, (total,))
 
-    def collect(first, last, again):
-        @pl.loop(0, 16)
+    def collect(groups, again):
+        per = 16 if again else 4
+
+        @pl.loop(0, 64 // per)
         def _(step):
-            for part in range(4):
-                chunk = step * 4 + part
-                (got,) = gather_sums([total], chunk * 2, rank_ref[pl.ds(chunk, 1), :], first, last)
+            for part in range(per):
+                chunk = step * per + part
+                (got,) = gather_sums([total], chunk * 2, rank_ref[pl.ds(chunk, 1), :], groups)
                 at = pl.ds(chunk, 1)
                 sums[at, :] = sums[at, :] + got if again else got
 
@@ -314,27 +322,29 @@
         near = jnp.full((1, 128), NEAR, F32)
         return jnp.concatenate([block[0:7], press, hinv, scale, near, jnp.zeros((5, 128), F32)], axis=0)
 
-    def own_fields(step, part):
-        lanes = pl.ds(pl.multiple_of(step * 512, 512) + 128 * part, 128)
-        return fields(own_ref[:, lanes], dens_ref[pl.ds(step * 4 + part, 1), :])
+    def own_fields(step, part, per):
+        lanes = pl.ds(pl.multiple_of(step * (128 * per), 128 * per) + 128 * part, 128)
+        return fields(own_ref[:, lanes], dens_ref[pl.ds(step * per + part, 1), :])
 
     @pl.loop(0, 16)
     def _(step):
         for part in range(4):
             chunk = step * 4 + part
             lanes = pl.ds(pl.multiple_of(step * 512, 512) + 128 * part, 128)
-            put_sources(sources, chunk * 2, own_fields(step, part))
+            put_sources(sources, chunk * 2, own_fields(step, part, 4))
             put_sources(sources, chunk * 2 + 128, fields(ghost_ref[:, lanes], gdens_ref[pl.ds(chunk, 1), :]))
 
-    def prepare(first, last, again):
-        @pl.loop(0, 16)
+    def prepare(groups, again):
+        per = 16 if again else 4
+
+        @pl.loop(0, 64 // per)
         def _(step):
-            for part in range(4):
-                chunk = step * 4 + part
-                put_targets(columns, chunk, own_fields(step, part), rank_ref[pl.ds(chunk, 1), :], first, last)
-                for g in range(first, last):
+            for part in range(per):
+                chunk = step * per + part
+                put_targets(columns, chunk, own_fields(step, part, per), rank_ref[pl.ds(chunk, 1), :], groups)
+                for g in groups:
                     for total in (ax, ay, az, heat):
-                        total[pl.ds(g * 1024 + chunk * 16, 16), :] = jnp.zeros((16, 128), F32)
+                        total[pl.ds(pl.multiple_of(g * 1024 + chunk * 16, 16), 16), :] = jnp.zeros((16, 128), F32)
 
     for_all_groups(most, prepare)
     sub = iota((16, 128), 0)
@@ -342,13 +352,15 @@
 
     run_items(number, code_ref, columns, sources, spread, 10, force_item, (ax, ay, az, heat))
 
-    def collect(first, last, again):
-        @pl.loop(0, 16)
+    def collect(groups, again):
+        per = 16 if again else 4
+
+        @pl.loop(0, 64 // per)
         def _(step):
-            for part in range(4):
-                chunk = step * 4 + part
-                got = gather_sums([ax, ay, az, heat], chunk * 2, rank_ref[pl.ds(chunk, 1), :], first, last)
-                lanes = pl.ds(pl.multiple_of(step * 512, 512) + 128 * part, 128)
+            for part in range(per):
+                chunk = step * per + part
+                got = gather_sums([ax, ay, az, heat], chunk * 2, rank_ref[pl.ds(chunk, 1), :], groups)
+                lanes = pl.ds(pl.multiple_of(step * (128 * per), 128 * per) + 128 * part, 128)
                 at = pl.ds(chunk, 1)
                 for n in range(3):
                     acc_ref[n : n + 1, lanes] = acc_ref[n : n + 1, lanes] + got[n] if again else got[n]

time: 80.4 us -> 80.4 us (level)
  no operation moved by 1% of the time
where the time goes in v5:
time: 80.4 us; the launch traced here: 80.2 us
  Pallas kernels  78.9 us (98%)
  between operations  1.3 us (2%)
    pallas_call x1, Pallas kernels, exchange(): pl.pallas_call(functools.partial(exchange_kernel, count_x, count_y), name...  37.1 us
    pallas_call x1, Pallas kernels, force_step(): pl.pallas_call(force_kernel, name='force', out_shape=(jax.ShapeDtypeStruc...  20.1 us
    pallas_call x1, Pallas kernels, density_step(): pl.pallas_call(density_kernel, name='density', out_shape=(jax.ShapeDtypeS...  12.8 us
    pallas_call x1, Pallas kernels, ghost_density_step(): pl.pallas_call(functools.partial(ghost_density_kernel, mesh.shape['gx'],...  8.85 us

profile of v5, /device:TPU:0, one launch (start us, length us, event | category | flops | bytes accessed | tf_op | source)
XLA Modules:
  0.0 80.2 jit_solution(13669933672712150989)
XLA Ops:
  1.3 37.1 %exchange.1 = (f32[8,8192]{1,0:T(8,128)S(1)}, f32[128,128]{1,0:T(8,128)S(1)}, f32[8,8192]{1,0:T(8,128)S(1)}, f32[8,320]{1,0:T(8,128)S(1)}, s32[8,1,1024]{2,1,0:T(1,128)S(1)}) custom-call(s32[1]{0:T(128)S(6)} %copy.11.used, s32[1,4]{1,0:T(1,128)} %bitcast.9, f32[8,8192]{1,0:T(8,128)} %particles_h.1, f32[64,128]{1,0:T(8,128)} %bitcast.7, s32[64,128]{1,0:T(8,128)} %bitcast.8, ...), custom_call_target="tpu_custom_call" | custom-call | tf_op jit(solution)/shard_map/exchange/pallas_call | solution.py:713
  38.4 12.8 %density.1 = (f32[64,128]{1,0:T(8,128)}, f32[64,128]{1,0:T(8,128)S(1)}, s32[8,384]{1,0:T(8,128)S(1)}, f32[64,128]{1,0:T(8,128)S(1)}) custom-call(f32[8,320]{1,0:T(8,128)S(1)} %get-tuple-element.14.cols_ref, f32[8,8192]{1,0:T(8,128)S(1)} %get-tuple-element.15.own_ref, f32[128,128]{1,0:T(8,128)S(1)} %get-tuple-element.16.extra_ref, ...), custom_call_target="tpu_custom_call" | custom-call | tf_op jit(solution)/shard_map/density/pallas_call | solution.py:377
  51.2 8.8 %ghost_density.1 = f32[8,8,128]{2,1,0:T(8,128)S(1)} custom-call(f32[64,128]{1,0:T(8,128)S(1)} %get-tuple-element.20.density.dens_ref, s32[8,1,1024]{2,1,0:T(1,128)S(1)} %get-tuple-element.21.exports_3), custom_call_target="tpu_custom_call" | custom-call | tf_op jit(solution)/shard_map/ghost_density/pallas_call | solution.py:798
  60.1 20.1 %force.1 = (f32[3,8192]{1,0:T(4,128)}, f32[64,128]{1,0:T(8,128)}) custom-call(s32[8,384]{1,0:T(8,128)S(1)} %get-tuple-element.19.code_ref, f32[8,8192]{1,0:T(8,128)S(1)} %get-tuple-element.15.own_ref, f32[8,8192]{1,0:T(8,128)S(1)} %get-tuple-element.17.ghost_ref, f32[64,128]{1,0:T(8,128)S(1)} %get-tuple-element.20.density.dens_ref, f32[64,128]{1,0:T(8,128)S(1)} %bitcast.6, ...), custom_call_target="tpu_custom_call" | custom-call | tf_op jit(solution)/shard_map/force/pallas_call | solution.py:403

commit v6 on v5

--- a/solution.py
+++ b/solution.py
@@ -275,7 +275,7 @@
     number, most = codes_s[0, STEPS - 1], codes_s[0, STEPS - 2]
 
     def prepare(groups, again):
-        per = 16 if again else 4
+        per = 16 if again else 8
 
         @pl.loop(0, 64 // per)
         def _(step):
@@ -291,7 +291,7 @@
     run_items(number, codes_s, columns, sources, spread, 4, density_item, (total,))
 
     def collect(groups, again):
-        per = 16 if again else 4
+        per = 16 if again else 8
 
         @pl.loop(0, 64 // per)
         def _(step):
@@ -335,7 +335,7 @@
             put_sources(sources, chunk * 2 + 128, fields(ghost_ref[:, lanes], gdens_ref[pl.ds(chunk, 1), :]))
 
     def prepare(groups, again):
-        per = 16 if again else 4
+        per = 16 if again else 8
 
         @pl.loop(0, 64 // per)
         def _(step):
@@ -353,7 +353,7 @@
     run_items(number, code_ref, columns, sources, spread, 10, force_item, (ax, ay, az, heat))
 
     def collect(groups, again):
-        per = 16 if again else 4
+        per = 16 if again else 8
 
         @pl.loop(0, 64 // per)
         def _(step):

time: 80.4 us -> 77.6 us (0.965)
  Pallas kernels: 78.9 us -> 75.7 us
    pallas_call x1, Pallas kernels: 12.8 us -> 11.1 us  [density_step(): pl.pallas_call(density_kernel, name='density', out_shape=(jax.ShapeDtypeS...]
    pallas_call x1, Pallas kernels: 20.1 us -> 18.6 us  [force_step(): pl.pallas_call(force_kernel, name='force', out_shape=(jax.ShapeDtypeStruc...]
where the time goes in v6:
time: 77.6 us; the launch traced here: 77 us
  Pallas kernels  75.7 us (98%)
  between operations  1.3 us (2%)
    pallas_call x1, Pallas kernels, exchange(): pl.pallas_call(functools.partial(exchange_kernel, count_x, count_y), name...  37.1 us
    pallas_call x1, Pallas kernels, force_step(): pl.pallas_call(force_kernel, name='force', out_shape=(jax.ShapeDtypeStruc...  18.6 us
    pallas_call x1, Pallas kernels, density_step(): pl.pallas_call(density_kernel, name='density', out_shape=(jax.ShapeDtypeS...  11.1 us
    pallas_call x1, Pallas kernels, ghost_density_step(): pl.pallas_call(functools.partial(ghost_density_kernel, mesh.shape['gx'],...  8.85 us

profile of v6, /device:TPU:0, one launch (start us, length us, event | category | flops | bytes accessed | tf_op | source)
XLA Modules:
  0.0 77.0 jit_solution(3016305189834079547)
XLA Ops:
  1.3 37.1 %exchange.1 = (f32[8,8192]{1,0:T(8,128)S(1)}, f32[128,128]{1,0:T(8,128)S(1)}, f32[8,8192]{1,0:T(8,128)S(1)}, f32[8,320]{1,0:T(8,128)S(1)}, s32[8,1,1024]{2,1,0:T(1,128)S(1)}) custom-call(s32[1]{0:T(128)S(6)} %copy.11.used, s32[1,4]{1,0:T(1,128)} %bitcast.9, f32[8,8192]{1,0:T(8,128)} %particles_h.1, f32[64,128]{1,0:T(8,128)} %bitcast.7, s32[64,128]{1,0:T(8,128)} %bitcast.8, ...), custom_call_target="tpu_custom_call" | custom-call | tf_op jit(solution)/shard_map/exchange/pallas_call | solution.py:713
  38.4 11.1 %density.1 = (f32[64,128]{1,0:T(8,128)}, f32[64,128]{1,0:T(8,128)S(1)}, s32[8,384]{1,0:T(8,128)S(1)}, f32[64,128]{1,0:T(8,128)S(1)}) custom-call(f32[8,320]{1,0:T(8,128)S(1)} %get-tuple-element.14.cols_ref, f32[8,8192]{1,0:T(8,128)S(1)} %get-tuple-element.15.own_ref, f32[128,128]{1,0:T(8,128)S(1)} %get-tuple-element.16.extra_ref, ...), custom_call_target="tpu_custom_call" | custom-call | tf_op jit(solution)/shard_map/density/pallas_call | solution.py:377
  49.5 8.8 %ghost_density.1 = f32[8,8,128]{2,1,0:T(8,128)S(1)} custom-call(f32[64,128]{1,0:T(8,128)S(1)} %get-tuple-element.20.density.dens_ref, s32[8,1,1024]{2,1,0:T(1,128)S(1)} %get-tuple-element.21.exports_3), custom_call_target="tpu_custom_call" | custom-call | tf_op jit(solution)/shard_map/ghost_density/pallas_call | solution.py:798
  58.4 18.6 %force.1 = (f32[3,8192]{1,0:T(4,128)}, f32[64,128]{1,0:T(8,128)}) custom-call(s32[8,384]{1,0:T(8,128)S(1)} %get-tuple-element.19.code_ref, f32[8,8192]{1,0:T(8,128)S(1)} %get-tuple-element.15.own_ref, f32[8,8192]{1,0:T(8,128)S(1)} %get-tuple-element.17.ghost_ref, f32[64,128]{1,0:T(8,128)S(1)} %get-tuple-element.20.density.dens_ref, f32[64,128]{1,0:T(8,128)S(1)} %bitcast.6, ...), custom_call_target="tpu_custom_call" | custom-call | tf_op jit(solution)/shard_map/force/pallas_call | solution.py:403
